TPU v7x, 512 devices: a whole 4x8x8 slice. The times are simulated.
512 devices in a mesh: ctx: 128 (over z, y, core), head: 4 (over x).
Axes of the slice: x: 4, y: 8, z: 8, core: 2. Of those that a mesh axis runs over, the one named last changes fastest.
Arguments:
- queries: bfloat16 [32768, 2048], P('ctx', 'head'), may hold values from -6 to 6
- keys: bfloat16 [32768, 2048], P('ctx', 'head'), may hold values from -6 to 6
- values: bfloat16 [32768, 2048], P('ctx', 'head'), may hold values from -6 to 6
- directions: bfloat16 [32768, 2048], P('ctx', 'head'), may hold values from -6 to 6
- rates: float32 [16, 32768], P('head', 'ctx'), may hold values from 0.004 to 1.996
- selected: int32 [256, 4], P('ctx'), may hold values from 0 to 255, as said below
- out_weight: bfloat16 [2048, 2048], P('head'), may hold values from -0.1875 to 0.1875
Outputs:
- projected: bfloat16 [32768, 2048], P('ctx', 'head')
Inputs may be any that keep to these rules, and one draw needn't show every extreme that they name: `selected`: row c lists query block c's key blocks: entry 0 is c itself; the others lie from max(c - 14, 0) to c - 1 (or are 0 when c is 0), may repeat, and the farthest distance 7 * 2 is reached in every draw.
All inputs are finite; a program needn't handle non-finite values.
Results may differ from a plain program's by a relative error of at most 0.022.
Values may be sent and summed in bfloat16 or wider, within the bound.
A program may use at most 64 MiB of HBM per device.

v0:
```python
import jax
import jax.numpy as jnp
from jax import lax
from jax.sharding import PartitionSpec as P

HEAD_DIM = 128
BLOCK = 128
LOOK = 7


def shifted(value, axis, by):
    count = lax.axis_size(axis)
    pairs = [(i, i + by) for i in range(count) if 0 <= i + by < count]
    return lax.ppermute(value, axis, pairs)


def product(left, right):
    return jnp.matmul(left, right, precision=lax.Precision.HIGHEST)


def flip_last(array):
    return jnp.swapaxes(array, -1, -2)


def block_terms(query_part, key_part, direction_part, rate_part):
    block_width = query_part.shape[-2]
    head_width = query_part.shape[-1]
    unit_vectors = direction_part * lax.rsqrt(
        jnp.sum(direction_part * direction_part, -1, keepdims=True) + 1e-06
    )
    positions = jnp.arange(block_width)
    strict_below = (positions[:, None] > positions[None, :]).astype(jnp.float32)
    at_or_below = (positions[:, None] >= positions[None, :]).astype(jnp.float32)
    identity = jnp.eye(block_width, dtype=jnp.float32)
    head_identity = jnp.eye(head_width, dtype=jnp.float32)
    gram_matrix = product(unit_vectors, flip_last(unit_vectors))
    lower_matrix = identity + rate_part[..., :, None] * gram_matrix * strict_below
    mixing = lax.linalg.triangular_solve(
        lower_matrix, rate_part[..., :, None] * identity, left_side=True, lower=True
    )
    query_proj = product(query_part, flip_last(unit_vectors)) * at_or_below
    key_proj = product(unit_vectors, flip_last(key_part)) * strict_below
    query_mix = product(query_proj, mixing)
    q_start = query_part - product(query_mix, unit_vectors)
    k_end = key_part - product(flip_last(product(mixing, key_proj)), unit_vectors)
    inner_scores = product(query_part, flip_last(key_part)) - product(query_mix, key_proj)
    block_maps = head_identity - product(product(flip_last(unit_vectors), mixing), unit_vectors)
    return (q_start, k_end, inner_scores, block_maps)


def body(queries, keys, values, directions, rates, selected, out_weight):
    local_tokens = queries.shape[0]
    heads_here = queries.shape[1] // HEAD_DIM
    blocks_here = local_tokens // BLOCK
    score_scale = HEAD_DIM ** (-0.5)

    def blocked(array):
        return array.reshape(blocks_here, BLOCK, heads_here, HEAD_DIM).transpose(0, 2, 1, 3)

    value_blocks = blocked(values)
    rate_blocks = rates.reshape(heads_here, blocks_here, BLOCK).transpose(1, 0, 2)
    q_start, k_end, inner_scores, block_maps = block_terms(
        blocked(queries).astype(jnp.float32),
        blocked(keys).astype(jnp.float32),
        blocked(directions).astype(jnp.float32),
        rate_blocks,
    )
    device = lax.axis_index("ctx")
    first_block = device * blocks_here
    positions = jnp.arange(BLOCK)
    causal = (positions[:, None] >= positions[None, :])[None]
    device_map = jnp.broadcast_to(
        jnp.eye(HEAD_DIM, dtype=jnp.float32), (heads_here, HEAD_DIM, HEAD_DIM)
    )
    tail_list = [None] * blocks_here
    for block_index in reversed(range(blocks_here)):
        tail_list[block_index] = product(k_end[block_index], flip_last(device_map))
        device_map = product(device_map, block_maps[block_index])
    key_tail = jnp.stack(tail_list)
    pieces = []
    front_list = []
    for query_block in range(blocks_here):
        listed = selected[query_block]
        entries = [
            (
                inner_scores[query_block] * score_scale,
                causal & jnp.any(listed == first_block + query_block),
                value_blocks[query_block],
            )
        ]
        moving = q_start[query_block]
        for earlier in reversed(range(query_block)):
            hit = jnp.any(listed == first_block + earlier)
            entries.append(
                (
                    product(moving, flip_last(k_end[earlier])) * score_scale,
                    jnp.broadcast_to(hit, (1, BLOCK, BLOCK)),
                    value_blocks[earlier],
                )
            )
            moving = product(moving, block_maps[earlier])
        pieces.append(entries)
        front_list.append(moving)
    query_front = jnp.stack(front_list)

    def score_rows(front, arrived_keys):
        front_rows = front.transpose(1, 0, 2, 3).reshape(heads_here, blocks_here * BLOCK, HEAD_DIM)
        key_rows = arrived_keys.transpose(1, 0, 2, 3).reshape(
            heads_here, blocks_here * BLOCK, HEAD_DIM
        )
        raw = product(front_rows, flip_last(key_rows)) * score_scale
        return raw.reshape(heads_here, blocks_here, BLOCK, blocks_here * BLOCK).transpose(
            1, 0, 2, 3
        )

    def collect(offset, front, arrived_keys, arrived_values):
        source_ids = (device - offset) * blocks_here + jnp.arange(blocks_here)
        hit = jnp.any(selected[:, :, None] == source_ids[None, None, :], axis=1)
        remote_scores = score_rows(front, arrived_keys)
        value_rows = arrived_values.transpose(1, 0, 2, 3).reshape(
            heads_here, blocks_here * BLOCK, HEAD_DIM
        )
        for query_block in range(blocks_here):
            allowed = jnp.repeat(hit[query_block], BLOCK)[None, None, :]
            pieces[query_block].append((remote_scores[query_block], allowed, value_rows))

    carried_keys = key_tail
    carried_values = value_blocks
    for offset in range(1, LOOK + 1):
        arrived_keys = shifted(carried_keys.astype(jnp.bfloat16), "ctx", 1).astype(
            carried_keys.dtype
        )
        arrived_values = shifted(carried_values, "ctx", 1)
        collect(offset, query_front, arrived_keys, arrived_values)
        if offset < LOOK:
            carried_keys = product(arrived_keys, flip_last(device_map)[None])
            carried_values = arrived_values
    outputs = []
    for query_block in range(blocks_here):
        entries = pieces[query_block]
        highest = None
        for scores, allowed, value_rows in entries:
            local_max = jnp.max(jnp.where(allowed, scores, -1e30), -1, keepdims=True)
            highest = local_max if highest is None else jnp.maximum(highest, local_max)
        expo_list = [
            jnp.exp(jnp.where(allowed, scores - highest, -1e30))
            for scores, allowed, value_rows in entries
        ]
        denominator = expo_list[0].sum(-1, keepdims=True)
        for expos in expo_list[1:]:
            denominator = denominator + expos.sum(-1, keepdims=True)
        blended = jnp.zeros((heads_here, BLOCK, HEAD_DIM), jnp.float32)
        for expos, entry in zip(expo_list, entries):
            weights = (expos / denominator).astype(jnp.bfloat16)
            blended = blended + jnp.einsum(
                "hqk,hke->hqe", weights, entry[2], preferred_element_type=jnp.float32
            )
        outputs.append(blended.astype(jnp.bfloat16))
    attended = jnp.stack(outputs)
    attended_flat = attended.transpose(0, 2, 1, 3).reshape(local_tokens, heads_here * HEAD_DIM)
    partial_value = jnp.dot(attended_flat, out_weight, preferred_element_type=jnp.float32).astype(
        jnp.bfloat16
    )
    summed = lax.psum_scatter(partial_value, "head", scatter_dimension=1, tiled=True).astype(
        jnp.float32
    )
    return summed.astype(jnp.bfloat16)


def solution(mesh):
    in_specs = (
        P("ctx", "head"),
        P("ctx", "head"),
        P("ctx", "head"),
        P("ctx", "head"),
        P("head", "ctx"),
        P("ctx", None),
        P("head", None),
    )
    out_specs = P("ctx", "head")
    return jax.shard_map(body, mesh=mesh, in_specs=in_specs, out_specs=out_specs, check_vma=False)
```

profile of v0, /device:TPU:8, one launch (start us, length us, event | category | flops | bytes accessed | tf_op | source)
XLA Modules:
  0.0 245.0 jit_solution(4442280766428890820)
XLA Ops:
  7.2 1.0 reshape.343
  8.2 1.1 reshape.369
  9.6 2.1 fusion.3
  11.6 79.2 %custom-call.3 = f32[2,4,1,128,128]{3,4,2,1,0:T(8,128)} custom-call(f32[2,4,1,128,128]{4,3,2,1,0:T(8,128)S(1)} %fusion.3), custom_call_target="InvertDiagBlocksLowerTriangular" | custom-call | tf_op jit(solution)/shard_map/triangular_solve | solution.py:38
  90.9 2.2 fusion.17
  93.8 1.2 fusion.111
  94.9 0.7 convolution_subtract_fusion.1
  96.1 1.0 fusion.150
  97.1 0.7 convolution_subtract_fusion
  99.2 0.7 pad_maximum_fusion
  100.0 1.9 collective-permute-start
  101.9 1.7 reshape.360
  103.6 1.7 copy.147
  105.3 3.8 %collective-permute-start.7 = (bf16[2,4,128,128]{3,2,1,0:T(8,128)(2,1)}, bf16[2,4,128,128]{3,2,1,0:T(8,128)(2,1)}, u32[]{:S(2)}, u32[]{:S(2)}) collective-permute-start(bf16[2,4,128,128]{3,2,1,0:T(8,128)(2,1)} %bitcast.449), channel_id=1, source_target_pairs={{0,4},{4,8},{8,12},{12,16},{16,20},{20,24},{24,28},{28,32},{32,36}... | collective-permute-start | bytes 786440 | tf_op jit(solution)/shard_map/ppermute | solution.py:14
  109.1 1.7 reshape.342
  110.8 2.1 fusion.41
  113.0 1.7 fusion.4
  114.6 1.0 fusion.149
  115.7 0.7 convolution_subtract_fusion.2
  116.5 1.1 convolution_bitcast_fusion.2
  118.7 1.0 convolution_subtract_fusion.3
  120.9 0.8 compare_reduce_fusion.9
  121.6 1.3 fusion.127
  123.4 1.1 maximum_bitcast_fusion
  124.5 1.2 select_reduce_fusion.14
  125.8 1.3 fusion.5
  127.1 1.9 collective-permute-start.1
  129.1 1.0 copy.67
  130.7 1.0 copy.78
  131.7 3.6 %collective-permute-start.8 = (bf16[2,4,128,128]{3,2,1,0:T(8,128)(2,1)}, bf16[2,4,128,128]{3,2,1,0:T(8,128)(2,1)S(1)}, u32[]{:S(2)}, u32[]{:S(2)}) collective-permute-start(bf16[2,4,128,128]{3,2,1,0:T(8,128)(2,1)} %collective-permute-done.7), channel_id=1, source_target_pairs={{0,4},{4,8},{8,12},{12,16},{16,20},{20,24},{24,28},{28,32},{32,36}... | collective-permute-start | bytes 786440 | tf_op jit(solution)/shard_map/ppermute | solution.py:14
  135.9 1.9 collective-permute-start.2
  138.5 1.1 collective-permute-done.8
  139.6 3.7 %collective-permute-start.9 = (bf16[2,4,128,128]{3,2,1,0:T(8,128)(2,1)S(1)}, bf16[2,4,128,128]{3,2,1,0:T(8,128)(2,1)S(1)}, u32[]{:S(2)}, u32[]{:S(2)}) collective-permute-start(bf16[2,4,128,128]{3,2,1,0:T(8,128)(2,1)S(1)} %collective-permute-done.8), channel_id=1, source_target_pairs={{0,4},{4,8},{8,12},{12,16},{16,20},{20,24},{24,28},{28,32},{32,36}... | collective-permute-start | bytes 786440 | tf_op jit(solution)/shard_map/ppermute | solution.py:14
  144.0 2.3 collective-permute-start.3
  147.3 4.1 %collective-permute-start.10 = (bf16[2,4,128,128]{3,2,1,0:T(8,128)(2,1)S(1)}, bf16[2,4,128,128]{3,2,1,0:T(8,128)(2,1)S(1)}, u32[]{:S(2)}, u32[]{:S(2)}) collective-permute-start(bf16[2,4,128,128]{3,2,1,0:T(8,128)(2,1)S(1)} %collective-permute-done.9), channel_id=1, source_target_pairs={{0,4},{4,8},{8,12},{12,16},{16,20},{20,24},{24,28},{28,32},{32,36}... | collective-permute-start | bytes 786440 | tf_op jit(solution)/shard_map/ppermute | solution.py:14
  152.1 2.3 collective-permute-start.4
  155.2 4.4 %collective-permute-start.11 = (bf16[2,4,128,128]{3,2,1,0:T(8,128)(2,1)S(1)}, bf16[2,4,128,128]{3,2,1,0:T(8,128)(2,1)S(1)}, u32[]{:S(2)}, u32[]{:S(2)}) collective-permute-start(bf16[2,4,128,128]{3,2,1,0:T(8,128)(2,1)S(1)} %collective-permute-done.10), channel_id=1, source_target_pairs={{0,4},{4,8},{8,12},{12,16},{16,20},{20,24},{24,28},{28,32},{32,36}... | collective-permute-start | bytes 786440 | tf_op jit(solution)/shard_map/ppermute | solution.py:14
  160.2 2.3 collective-permute-start.5
  163.2 4.6 %collective-permute-start.12 = (bf16[2,4,128,128]{3,2,1,0:T(8,128)(2,1)S(1)}, bf16[2,4,128,128]{3,2,1,0:T(8,128)(2,1)S(1)}, u32[]{:S(2)}, u32[]{:S(2)}) collective-permute-start(bf16[2,4,128,128]{3,2,1,0:T(8,128)(2,1)S(1)} %collective-permute-done.11), channel_id=1, source_target_pairs={{0,4},{4,8},{8,12},{12,16},{16,20},{20,24},{24,28},{28,32},{32,36}... | collective-permute-start | bytes 786440 | tf_op jit(solution)/shard_map/ppermute | solution.py:14
  168.5 2.1 collective-permute-start.6
  171.3 4.4 %collective-permute-start.13 = (bf16[2,4,128,128]{3,2,1,0:T(8,128)(2,1)S(1)}, bf16[2,4,128,128]{3,2,1,0:T(8,128)(2,1)S(1)}, u32[]{:S(2)}, u32[]{:S(2)}) collective-permute-start(bf16[2,4,128,128]{3,2,1,0:T(8,128)(2,1)S(1)} %collective-permute-done.12), channel_id=1, source_target_pairs={{0,4},{4,8},{8,12},{12,16},{16,20},{20,24},{24,28},{28,32},{32,36}... | collective-permute-start | bytes 786440 | tf_op jit(solution)/shard_map/ppermute | solution.py:14
  177.1 0.9 fusion.27
  178.0 1.1 fusion.26
  179.8 1.2 fusion.112
  181.0 1.7 convolution_add_fusion.7
  182.8 1.2 fusion.121
  188.9 1.7 convolution_convert_fusion
  190.7 47.5 %reduce-scatter.2.cloned.1.call-done = bf16[256,512]{1,0:T(8,128)(2,1)} async-done(((bf16[256,2048]{1,0:T(8,128)(2,1)}), bf16[256,512]{1,0:T(8,128)(2,1)}) %reduce-scatter.2.cloned.1.call-update) | async-done | bytes 262160 | tf_op jit(solution)/shard_map/reduce_scatter | solution.py:164
  (139 shorter events, 20.5 us)
Async XLA Ops:
  6.5 182.4 %copy-start = (bf16[512,2048]{1,0:T(8,128)(2,1)S(1)}, bf16[512,2048]{1,0:T(8,128)(2,1)}, u32[]{:S(2)}) copy-start(bf16[512,2048]{1,0:T(8,128)(2,1)} %param.13) | copy-start | bytes 6291460
  6.5 84.4 %copy-start.13 = (f32[4,256]{1,0:T(4,128)S(1)}, f32[4,256]{1,0:T(4,128)}, u32[]{:S(2)}) copy-start(f32[4,256]{1,0:T(4,128)} %param.11) | copy-start | bytes 12292
  6.5 231.6 %reduce-scatter.2.cloned.1.call-start = ((), (), s32[]{:S(2)}) async-start(), calls=%async_computation.1 | async-start | bytes 1310720 | tf_op jit(solution)/shard_map/reduce_scatter | solution.py:164
  93.8 3.3 %copy-start.1 = (f32[2,4,128,128]{3,2,1,0:T(8,128)}, f32[2,4,128,128]{3,2,1,0:T(8,128)S(1)}, u32[]{:S(2)}) copy-start(f32[2,4,128,128]{3,2,1,0:T(8,128)S(1)} %convolution_multiply_fusion.8) | copy-start | bytes 1572868
  95.7 2.9 %copy-start.4 = (f32[2,4,128,128]{3,2,1,0:T(8,128)}, f32[2,4,128,128]{3,2,1,0:T(8,128)S(1)}, u32[]{:S(2)}) copy-start(f32[2,4,128,128]{3,2,1,0:T(8,128)S(1)} %convolution_subtract_fusion.1) | copy-start | bytes 1572868
  96.1 3.1 %copy-start.10 = (f32[4,128,128]{2,1,0:T(8,128)}, f32[4,128,128]{2,1,0:T(8,128)S(1)}, u32[]{:S(2)}) copy-start(f32[4,128,128]{2,1,0:T(8,128)S(1)} %fusion.38) | copy-start | bytes 786436
  97.9 1.4 copy-start.6
  100.0 25.8 %collective-permute-start = (bf16[2,4,128,128]{3,2,1,0:T(8,128)(2,1)}, bf16[2,4,128,128]{3,2,1,0:T(8,128)(2,1)}, u32[]{:S(2)}, u32[]{:S(2)}) collective-permute-start(bf16[2,4,128,128]{3,2,1,0:T(8,128)(2,1)} %pad_maximum_fusion), channel_id=1, source_target_pairs={{0,4},{4,8},{8,12},{12,16},{16,20},{20,24},{24,28},{28,32},{32,36}... | collective-permute-start | bytes 786440 | tf_op jit(solution)/shard_map/ppermute | solution.py:14
  105.3 25.4 %collective-permute-start.7 = (bf16[2,4,128,128]{3,2,1,0:T(8,128)(2,1)}, bf16[2,4,128,128]{3,2,1,0:T(8,128)(2,1)}, u32[]{:S(2)}, u32[]{:S(2)}) collective-permute-start(bf16[2,4,128,128]{3,2,1,0:T(8,128)(2,1)} %bitcast.449), channel_id=1, source_target_pairs={{0,4},{4,8},{8,12},{12,16},{16,20},{20,24},{24,28},{28,32},{32,36}... | collective-permute-start | bytes 786440 | tf_op jit(solution)/shard_map/ppermute | solution.py:14
  112.9 2.8 %copy-start.3 = (bf16[2,128,4,128]{3,2,1,0:T(4,128)(2,1)S(1)}, bf16[2,128,4,128]{3,2,1,0:T(4,128)(2,1)}, u32[]{:S(2)}) copy-start(bf16[2,128,4,128]{3,2,1,0:T(4,128)(2,1)} %reshape.342) | copy-start | bytes 786436
  113.0 3.5 %copy-start.5 = (f32[2,4,128,128]{3,2,1,0:T(8,128)S(1)}, f32[2,4,128,128]{3,2,1,0:T(8,128)}, u32[]{:S(2)}) copy-start(f32[2,4,128,128]{3,2,1,0:T(8,128)} %copy-done.4) | copy-start | bytes 1572868
  114.6 3.7 %copy-start.11 = (f32[4,128,128]{2,1,0:T(8,128)S(1)}, f32[4,128,128]{2,1,0:T(8,128)}, u32[]{:S(2)}) copy-start(f32[4,128,128]{2,1,0:T(8,128)} %copy-done.10) | copy-start | bytes 786436
  115.7 3.0 %copy-start.2 = (f32[2,4,128,128]{3,2,1,0:T(8,128)S(1)}, f32[2,4,128,128]{3,2,1,0:T(8,128)}, u32[]{:S(2)}) copy-start(f32[2,4,128,128]{3,2,1,0:T(8,128)} %copy-done.1) | copy-start | bytes 1572868
  115.7 3.0 %copy-start.12 = (f32[2,4,128,128]{2,3,1,0:T(8,128)S(1)}, f32[2,4,128,128]{2,3,1,0:T(8,128)}, u32[]{:S(2)}) copy-start(f32[2,4,128,128]{2,3,1,0:T(8,128)} %fusion.41) | copy-start | bytes 1572868
  116.5 2.3 copy-start.8
  116.5 3.4 %copy-start.14 = (s32[2,4]{1,0:T(2,128)S(1)}, s32[2,4]{1,0:T(2,128)}, u32[]{:S(2)}) copy-start(s32[2,4]{1,0:T(2,128)} %param.12) | copy-start | bytes 100
  118.7 5.8 %copy-start.7 = (f32[2,4,128,128]{3,2,1,0:T(8,128)S(1)}, f32[2,4,128,128]{3,2,1,0:T(8,128)}, u32[]{:S(2)}) copy-start(f32[2,4,128,128]{3,2,1,0:T(8,128)} %copy-done.6) | copy-start | bytes 1572868
  123.2 1.3 copy-start.9
  127.1 8.4 %collective-permute-start.1 = (bf16[2,4,128,128]{3,2,0,1:T(8,128)(2,1)S(1)}, bf16[2,4,128,128]{3,2,0,1:T(8,128)(2,1)S(1)}, u32[]{:S(2)}, u32[]{:S(2)}) collective-permute-start(bf16[2,4,128,128]{3,2,0,1:T(8,128)(2,1)S(1)} %fusion.5), channel_id=1, source_target_pairs={{0,4},{4,8},{8,12},{12,16},{16,20},{20,24},{24,28},{28,32},{32,36}... | collective-permute-start | bytes 786440 | tf_op jit(solution)/shard_map/ppermute | solution.py:14
  131.7 7.9 %collective-permute-start.8 = (bf16[2,4,128,128]{3,2,1,0:T(8,128)(2,1)}, bf16[2,4,128,128]{3,2,1,0:T(8,128)(2,1)S(1)}, u32[]{:S(2)}, u32[]{:S(2)}) collective-permute-start(bf16[2,4,128,128]{3,2,1,0:T(8,128)(2,1)} %collective-permute-done.7), channel_id=1, source_target_pairs={{0,4},{4,8},{8,12},{12,16},{16,20},{20,24},{24,28},{28,32},{32,36}... | collective-permute-start | bytes 786440 | tf_op jit(solution)/shard_map/ppermute | solution.py:14
  135.9 7.7 %collective-permute-start.2 = (bf16[2,4,128,128]{3,2,0,1:T(8,128)(2,1)S(1)}, bf16[2,4,128,128]{3,2,0,1:T(8,128)(2,1)S(1)}, u32[]{:S(2)}, u32[]{:S(2)}) collective-permute-start(bf16[2,4,128,128]{3,2,0,1:T(8,128)(2,1)S(1)} %fusion.6), channel_id=1, source_target_pairs={{0,4},{4,8},{8,12},{12,16},{16,20},{20,24},{24,28},{28,32},{32,36}... | collective-permute-start | bytes 786440 | tf_op jit(solution)/shard_map/ppermute | solution.py:14
  139.6 7.7 %collective-permute-start.9 = (bf16[2,4,128,128]{3,2,1,0:T(8,128)(2,1)S(1)}, bf16[2,4,128,128]{3,2,1,0:T(8,128)(2,1)S(1)}, u32[]{:S(2)}, u32[]{:S(2)}) collective-permute-start(bf16[2,4,128,128]{3,2,1,0:T(8,128)(2,1)S(1)} %collective-permute-done.8), channel_id=1, source_target_pairs={{0,4},{4,8},{8,12},{12,16},{16,20},{20,24},{24,28},{28,32},{32,36}... | collective-permute-start | bytes 786440 | tf_op jit(solution)/shard_map/ppermute | solution.py:14
  144.0 7.7 %collective-permute-start.3 = (bf16[2,4,128,128]{3,2,0,1:T(8,128)(2,1)S(1)}, bf16[2,4,128,128]{3,2,0,1:T(8,128)(2,1)S(1)}, u32[]{:S(2)}, u32[]{:S(2)}) collective-permute-start(bf16[2,4,128,128]{3,2,0,1:T(8,128)(2,1)S(1)} %fusion.7), channel_id=1, source_target_pairs={{0,4},{4,8},{8,12},{12,16},{16,20},{20,24},{24,28},{28,32},{32,36}... | collective-permute-start | bytes 786440 | tf_op jit(solution)/shard_map/ppermute | solution.py:14
  147.3 7.8 %collective-permute-start.10 = (bf16[2,4,128,128]{3,2,1,0:T(8,128)(2,1)S(1)}, bf16[2,4,128,128]{3,2,1,0:T(8,128)(2,1)S(1)}, u32[]{:S(2)}, u32[]{:S(2)}) collective-permute-start(bf16[2,4,128,128]{3,2,1,0:T(8,128)(2,1)S(1)} %collective-permute-done.9), channel_id=1, source_target_pairs={{0,4},{4,8},{8,12},{12,16},{16,20},{20,24},{24,28},{28,32},{32,36}... | collective-permute-start | bytes 786440 | tf_op jit(solution)/shard_map/ppermute | solution.py:14
  152.1 7.7 %collective-permute-start.4 = (bf16[2,4,128,128]{3,2,0,1:T(8,128)(2,1)S(1)}, bf16[2,4,128,128]{3,2,0,1:T(8,128)(2,1)S(1)}, u32[]{:S(2)}, u32[]{:S(2)}) collective-permute-start(bf16[2,4,128,128]{3,2,0,1:T(8,128)(2,1)S(1)} %fusion.8), channel_id=1, source_target_pairs={{0,4},{4,8},{8,12},{12,16},{16,20},{20,24},{24,28},{28,32},{32,36}... | collective-permute-start | bytes 786440 | tf_op jit(solution)/shard_map/ppermute | solution.py:14
  155.2 8.0 %collective-permute-start.11 = (bf16[2,4,128,128]{3,2,1,0:T(8,128)(2,1)S(1)}, bf16[2,4,128,128]{3,2,1,0:T(8,128)(2,1)S(1)}, u32[]{:S(2)}, u32[]{:S(2)}) collective-permute-start(bf16[2,4,128,128]{3,2,1,0:T(8,128)(2,1)S(1)} %collective-permute-done.10), channel_id=1, source_target_pairs={{0,4},{4,8},{8,12},{12,16},{16,20},{20,24},{24,28},{28,32},{32,36}... | collective-permute-start | bytes 786440 | tf_op jit(solution)/shard_map/ppermute | solution.py:14
  160.2 7.9 %collective-permute-start.5 = (bf16[2,4,128,128]{3,2,0,1:T(8,128)(2,1)S(1)}, bf16[2,4,128,128]{3,2,0,1:T(8,128)(2,1)S(1)}, u32[]{:S(2)}, u32[]{:S(2)}) collective-permute-start(bf16[2,4,128,128]{3,2,0,1:T(8,128)(2,1)S(1)} %fusion.9), channel_id=1, source_target_pairs={{0,4},{4,8},{8,12},{12,16},{16,20},{20,24},{24,28},{28,32},{32,36}... | collective-permute-start | bytes 786440 | tf_op jit(solution)/shard_map/ppermute | solution.py:14
  163.2 8.0 %collective-permute-start.12 = (bf16[2,4,128,128]{3,2,1,0:T(8,128)(2,1)S(1)}, bf16[2,4,128,128]{3,2,1,0:T(8,128)(2,1)S(1)}, u32[]{:S(2)}, u32[]{:S(2)}) collective-permute-start(bf16[2,4,128,128]{3,2,1,0:T(8,128)(2,1)S(1)} %collective-permute-done.11), channel_id=1, source_target_pairs={{0,4},{4,8},{8,12},{12,16},{16,20},{20,24},{24,28},{28,32},{32,36}... | collective-permute-start | bytes 786440 | tf_op jit(solution)/shard_map/ppermute | solution.py:14
  168.5 7.7 %collective-permute-start.6 = (bf16[2,4,128,128]{3,2,0,1:T(8,128)(2,1)S(1)}, bf16[2,4,128,128]{3,2,0,1:T(8,128)(2,1)S(1)}, u32[]{:S(2)}, u32[]{:S(2)}) collective-permute-start(bf16[2,4,128,128]{3,2,0,1:T(8,128)(2,1)S(1)} %fusion.10), channel_id=1, source_target_pairs={{0,4},{4,8},{8,12},{12,16},{16,20},{20,24},{24,28},{28,32},{32,36}... | collective-permute-start | bytes 786440 | tf_op jit(solution)/shard_map/ppermute | solution.py:14
  171.3 11.4 %collective-permute-start.13 = (bf16[2,4,128,128]{3,2,1,0:T(8,128)(2,1)S(1)}, bf16[2,4,128,128]{3,2,1,0:T(8,128)(2,1)S(1)}, u32[]{:S(2)}, u32[]{:S(2)}) collective-permute-start(bf16[2,4,128,128]{3,2,1,0:T(8,128)(2,1)S(1)} %collective-permute-done.12), channel_id=1, source_target_pairs={{0,4},{4,8},{8,12},{12,16},{16,20},{20,24},{24,28},{28,32},{32,36}... | collective-permute-start | bytes 786440 | tf_op jit(solution)/shard_map/ppermute | solution.py:14
Sparse Core Ops, SparseCore 0:
  190.8 47.3 reduce-scatter.1
where the time goes:
time: 246 us; the launch traced here: 245 us
  other arithmetic  88.5 us (36%)
  waiting for transfers between devices  49.1 us (20%)
  starting transfers between devices  43.4 us (18%)
  matrix products  37.2 us (15%)
  between operations  14.4 us (6%)
  local copies, waits for them, and re-layouts  12.4 us (5%)
    another operation x1, other arithmetic, block_terms(): lax.linalg.triangular_solve(lower_matrix, rate_part[..., :, None] * ident...  79.2 us
    reduce_scatter x1, waiting for transfers between devices, body(): lax.psum_scatter(partial_value, 'head', scatter_dimension=1, tiled=True)  47.5 us
    ppermute x14, starting transfers between devices, shifted(): return lax.ppermute(value, axis, pairs)  43.4 us
    dot_general x30, matrix products, product(): return jnp.matmul(left, right, precision=lax.Precision.HIGHEST)  24.6 us
    dot_general x17, matrix products, body(): jnp.einsum('hqk,hke->hqe', weights, entry[2], preferred_element_type=jnp....  8.66 us
    reshape x4, local copies, waits for them, and re-layouts, blocked(): array.reshape(blocks_here, BLOCK, heads_here, HEAD_DIM)  6.17 us
  transfers between devices with their start and end apart: 15, of which 4 were waited for; matrix products, arithmetic and copies ran while one was open for 15% of the time, Pallas kernels for 0%

commit v1 on v0

v1 whole, which is shorter than its diff:
```python
import functools

import jax
import jax.numpy as jnp
from jax import lax
from jax.experimental import pallas as pl
from jax.experimental.pallas import tpu as pltpu
from jax.sharding import PartitionSpec as P

MESH = pl.DeviceIdType.MESH
HD = 128
B = 128
HEADS = 4
HOPS = 3
NEG = -1e30
SCALE = HD ** (-0.5)
f32 = jnp.float32
bf16 = jnp.bfloat16
NN = (((1,), (0,)), ((), ()))
NT = (((1,), (1,)), ((), ()))
TN = (((0,), (0,)), ((), ()))


def dot(a, b, dims):
    return lax.dot_general(a, b, dims, preferred_element_type=f32)


def split(a):
    high = a.astype(bf16)
    return high, (a - high.astype(f32)).astype(bf16)


def dot3(a, b, dims):
    return dot(a[0], b[0], dims) + (dot(a[1], b[0], dims) + dot(a[0], b[1], dims))


def dot_left(a, b, dims):
    return dot(a[0], b, dims) + dot(a[1], b, dims)


def dot_right(a, b, dims):
    return dot(a, b[0], dims) + dot(a, b[1], dims)


def block_terms(q, k, w, beta, hooks):
    each = range(len(q))
    row = lax.broadcasted_iota(jnp.int32, (B, B), 0)
    col = lax.broadcasted_iota(jnp.int32, (B, B), 1)
    eye = (row == col).astype(f32)
    grams = [
        dot(jnp.concatenate([w[i], q[i]], 0), jnp.concatenate([w[i], k[i]], 0), NT) for i in each
    ]
    wide = [w[i].astype(f32) for i in each]
    norm = [jnp.sum(wide[i] * wide[i], -1, keepdims=True) for i in each]
    rate = [
        jnp.transpose(jnp.broadcast_to(beta[i], (B, B))) / (norm[i] + 1e-6) for i in each
    ]
    lower = [jnp.where(row > col, rate[i] * grams[i][:B, :B], 0.0) for i in each]
    key_proj = [split(jnp.where(row > col, grams[i][:B, B:], 0.0)) for i in each]
    query_proj = [split(jnp.where(row >= col, grams[i][B:, :B], 0.0)) for i in each]

    def off_diagonal(size):
        return ((row ^ col) < 2 * size) & ((row & size) != 0) & ((col & size) == 0)

    inverse = [eye - jnp.where(off_diagonal(1), lower[i], 0.0) for i in each]
    size = 2
    while size < B:
        mask = off_diagonal(size)
        parts = [split(inverse[i]) for i in each]
        below = [split(jnp.where(mask, lower[i], 0.0)) for i in each]
        step = [split(dot3(below[i], parts[i], NN)) for i in each]
        inverse = [inverse[i] - dot3(parts[i], step[i], NN) for i in each]
        if size in hooks:
            hooks[size]()
        size *= 2
    mixing = [split(inverse[i] * jnp.transpose(rate[i])) for i in each]
    mix_w = [split(dot_left(mixing[i], w[i], NN)) for i in each]
    mix_k = [split(dot3(mixing[i], key_proj[i], NN)) for i in each]
    block_map = [eye - dot_right(w[i], mix_w[i], TN) for i in each]
    k_end = [k[i].astype(f32) - dot_left(mix_k[i], w[i], TN) for i in each]
    q_start = [q[i].astype(f32) - dot3(query_proj[i], mix_w[i], NN) for i in each]
    inner = [grams[i][B:, B:] - dot3(query_proj[i], mix_k[i], NN) for i in each]
    return q_start, k_end, inner, block_map


def kernel(
    n_ctx, sel, q_ref, k_ref, v_ref, w_ref, rate_ref, ow_ref, out_ref,
    k_own, k_par, k_ext, v_own, v_par, v_ext, k_stage, k_tail, d_mine, d_part,
    q_front, q_chip, m_ref, l_ref, acc_ref, local, att, wfull,
    sv, rv, svp, rvp, sve, rve, sk, rk, skp, rkp, ske, rke, sd, rd, sw, rw, swp, rwp, sa, ra, lw,
):
    me = lax.axis_index("ctx")
    x = lax.axis_index("head")
    core = lax.rem(me, 2)
    is0 = core == 0
    is1 = core == 1
    n_x = 4
    nxt = lax.rem(me + 2, n_ctx)
    prv = lax.rem(me + n_ctx - 2, n_ctx)
    partner = me + 1 - 2 * core
    cross = jnp.where(is0, lax.rem(me + n_ctx - 1, n_ctx), lax.rem(me + 1, n_ctx))
    lanes = [slice(h * HD, (h + 1) * HD) for h in range(HEADS)]
    rows = [slice(n * B, (n + 1) * B) for n in range(2)]

    def remote(src, dst, ss, rs, to):
        return pltpu.make_async_remote_copy(
            src_ref=src, dst_ref=dst, send_sem=ss, recv_sem=rs, device_id=to, device_id_type=MESH
        )

    barrier = pltpu.get_barrier_semaphore()
    for other in (nxt, prv, partner, cross):
        pl.semaphore_signal(barrier, inc=1, device_id=(other, x), device_id_type=MESH)
    for r in range(1, n_x):
        pl.semaphore_signal(
            barrier, inc=1, device_id=(me, lax.rem(x + r, n_x)), device_id_type=MESH
        )
    pl.semaphore_wait(barrier, 7)

    def v_hop(s, h):
        src = v_ref.at[:, lanes[h]] if s == 0 else v_own.at[s - 1, :, lanes[h]]
        return remote(src, v_own.at[s, :, lanes[h]], sv.at[s, h], rv.at[s, h], (nxt, x))

    def k_hop(s, h):
        return remote(
            k_stage.at[s, :, lanes[h]], k_own.at[s, :, lanes[h]], sk.at[s, h], rk.at[s, h], (nxt, x)
        )

    def v_share(s, h):
        return remote(
            v_own.at[s, :, lanes[h]], v_par.at[s, :, lanes[h]], svp.at[s, h], rvp.at[s, h], (partner, x)
        )

    def k_share(s, h):
        return remote(
            k_own.at[s, :, lanes[h]], k_par.at[s, :, lanes[h]], skp.at[s, h], rkp.at[s, h], (partner, x)
        )

    def v_extra(h, src, to):
        return remote(src.at[:, lanes[h]], v_ext.at[:, lanes[h]], sve.at[h], rve.at[h], (to, x))

    def k_extra(h, src, to):
        return remote(src.at[:, lanes[h]], k_ext.at[:, lanes[h]], ske.at[h], rke.at[h], (to, x))

    half = pl.ds(pl.multiple_of(core * 256, 256), 256)

    def w_send(r):
        to = lax.rem(x + r, n_x)
        cols = pl.ds(pl.multiple_of(to * 512, 512), 512)
        return remote(ow_ref.at[half, cols], wfull.at[x, half], sw.at[r - 1], rw.at[r - 1], (me, to))

    def w_recv(r):
        src = lax.rem(x + n_x - r, n_x)
        return remote(wfull.at[src, half], wfull.at[src, half], sw.at[r - 1], rw.at[r - 1], (me, src))

    def w_share(r):
        src = lax.rem(x + n_x - r, n_x)
        return remote(
            wfull.at[src, half], wfull.at[src, half], swp.at[r - 1], rwp.at[r - 1], (partner, x)
        )

    other_half = pl.ds(pl.multiple_of((1 - core) * 256, 256), 256)

    def w_shared(r):
        src = lax.rem(x + n_x - r, n_x)
        return remote(
            wfull.at[src, other_half], wfull.at[src, other_half], swp.at[r - 1], rwp.at[r - 1],
            (partner, x),
        )

    def a_send(r, h):
        to = lax.rem(x + r, n_x)
        slot = att.at[x, :, lanes[h]]
        return remote(slot, slot, sa.at[r - 1, h], ra.at[r - 1, h], (me, to))

    def a_recv(r, h):
        src = lax.rem(x + n_x - r, n_x)
        slot = att.at[src, :, lanes[h]]
        return remote(slot, slot, sa.at[r - 1, h], ra.at[r - 1, h], (me, src))

    own_w = pltpu.make_async_copy(
        ow_ref.at[:, pl.ds(pl.multiple_of(x * 512, 512), 512)], wfull.at[x], lw
    )

    for h in range(HEADS):
        v_hop(0, h).start()
    for r in range(1, n_x):
        w_send(r).start()
    own_w.start()

    @pl.when(is0)
    def _():
        for h in range(HEADS):
            v_extra(h, v_ref, partner).start()

    def pass_value(s, h):
        v_hop(s, h).wait_recv()
        v_share(s, h).start()
        if s < HOPS - 1:
            v_hop(s + 1, h).start()
        else:

            @pl.when(is1)
            def _():
                v_extra(h, v_own.at[HOPS - 1], cross).start()

    pairs = [(n, h) for h in range(HEADS) for n in range(2)]

    def cut(ref):
        return [ref[rows[n], lanes[h]] for n, h in pairs]

    hooks = {64: lambda: pass_value(0, 0)}
    q_start, k_end, inner, block_map = block_terms(
        cut(q_ref), cut(k_ref), cut(w_ref),
        [rate_ref[h : h + 1, rows[n]] for n, h in pairs], hooks,
    )
    maps = [split(m) for m in block_map]
    tails, fronts = [], []
    for h in range(HEADS):
        d_mine[:, lanes[h]] = dot3(maps[2 * h + 1], maps[2 * h], NN)
    exchange_d = remote(d_mine, d_part, sd, rd, (partner, x))
    exchange_d.start()
    for h in range(HEADS):
        first, second = 2 * h, 2 * h + 1
        early = split(k_end[first])
        tails.append(
            jnp.concatenate([dot3(early, maps[second], NT), k_end[second]], 0)
        )
        late = split(q_start[second])
        fronts.append(jnp.concatenate([q_start[first], dot3(late, maps[first], NN)], 0))
        q_front[:, lanes[h]] = (fronts[h] * SCALE).astype(bf16)
        k_tail[:, lanes[h]] = tails[h].astype(bf16)
        local[h, B:, :B] = dot3(late, early, NT) * SCALE
        local[h, :B, :B] = inner[first] * SCALE
        local[h, B:, B:] = inner[second] * SCALE

    @pl.when(is0)
    def _():
        for h in range(HEADS):
            k_extra(h, k_tail, partner).start()

    for h in range(1, HEADS):
        pass_value(0, h)
    exchange_d.wait_recv()
    chip_maps = []
    for h in range(HEADS):
        d_own = d_mine[:, lanes[h]]
        d_other = d_part[:, lanes[h]]
        other = split(d_other)
        carried = dot3(split(tails[h]), other, NT)
        k_stage[0, :, lanes[h]] = jnp.where(is0, carried, tails[h]).astype(bf16)
        k_hop(0, h).start()
        front = fronts[h]
        moved = dot3(split(front), other, NN)
        q_chip[:, lanes[h]] = (jnp.where(is0, front, moved) * SCALE).astype(bf16)
        later = jnp.where(is0, d_other, d_own)
        sooner = jnp.where(is0, d_own, d_other)
        chip_maps.append(split(dot3(split(later), split(sooner), NN)))

    def bias(n, block):
        hit = sel[n, 0] == block
        for e in range(1, 4):
            hit = hit | (sel[n, e] == block)
        return jnp.where(hit, 0.0, NEG).astype(f32)

    def first_block(h):
        row = lax.broadcasted_iota(jnp.int32, (B, B), 0)
        col = lax.broadcasted_iota(jnp.int32, (B, B), 1)
        for n in range(2):
            tiles = [local[h, rows[n], rows[b]] + bias(n, 2 * me + b) for b in range(n)]
            tiles.append(
                jnp.where(row >= col, local[h, rows[n], rows[n]] + bias(n, 2 * me + n), NEG)
            )
            top = functools.reduce(jnp.maximum, tiles)
            top = jnp.broadcast_to(jnp.max(top, -1, keepdims=True), (B, B))
            expos = [jnp.exp(t - top) for t in tiles]
            m_ref[h, rows[n], :] = top
            l_ref[h, rows[n], :] = functools.reduce(jnp.add, expos)
            total = jnp.zeros((B, HD), f32)
            for b, e in enumerate(expos):
                total = total + dot(e.astype(bf16), v_ref[rows[b], lanes[h]], NN)
            acc_ref[h, rows[n], :] = total

    def attend(h, query, sources):
        scores = [dot(query, keys, NT) for keys, _, _ in sources]
        for n in range(2):
            tiles = [
                scores[i][rows[n], rows[b]] + bias(n, 2 * device + b)
                for i, (_, _, device) in enumerate(sources)
                for b in range(2)
            ]
            old = m_ref[h, rows[n], :]
            top = functools.reduce(jnp.maximum, tiles)
            top = jnp.maximum(old, jnp.max(top, -1, keepdims=True))
            fade = jnp.exp(old - top)
            expos = [jnp.exp(t - top) for t in tiles]
            m_ref[h, rows[n], :] = top
            l_ref[h, rows[n], :] = l_ref[h, rows[n], :] * fade + functools.reduce(jnp.add, expos)
            total = acc_ref[h, rows[n], :] * fade
            for i, (_, values, _) in enumerate(sources):
                weights = jnp.concatenate(expos[2 * i : 2 * i + 2], 1).astype(bf16)
                total = total + dot(weights, values, NN)
            acc_ref[h, rows[n], :] = total

    def attend_extra(h):
        v_extra(h, v_own.at[HOPS - 1], cross).wait_recv()
        k_extra(h, k_tail, cross).wait_recv()
        device = jnp.where(is1, me - 1, me - 7)
        attend(h, q_front[:, lanes[h]], [(k_ext[:, lanes[h]], v_ext[:, lanes[h]], device)])

    def attend_hop(s, h):
        v_share(s, h).wait_recv()
        k_share(s, h).wait_recv()
        own = me - 2 * (s + 1)
        attend(
            h,
            q_chip[:, lanes[h]],
            [
                (k_own[s, :, lanes[h]], v_own[s, :, lanes[h]], own),
                (k_par[s, :, lanes[h]], v_par[s, :, lanes[h]], own + 1 - 2 * core),
            ],
        )

    def finish(h):
        total = jnp.sum(l_ref[h], -1, keepdims=True)
        att[x, :, lanes[h]] = (acc_ref[h] / total).astype(bf16)
        for r in range(1, n_x):
            a_send(r, h).start()

    def pass_key(s, h):
        k_hop(s, h).wait_recv()
        k_share(s, h).start()

        def forward():
            k_stage[s + 1, :, lanes[h]] = dot_right(k_own[s, :, lanes[h]], chip_maps[h], NT).astype(bf16)

        if s < HOPS - 1:
            forward()
            k_hop(s + 1, h).start()
        else:

            @pl.when(is1)
            def _():
                forward()
                k_extra(h, k_stage.at[HOPS], cross).start()

    for h in range(HEADS):
        first_block(h)

    @pl.when(is1)
    def _():
        for h in range(HEADS):
            attend_extra(h)

    for r in range(1, n_x):
        w_recv(r).wait_recv()
        w_share(r).start()
    for s in range(HOPS):
        if s + 1 < HOPS:
            for h in range(HEADS):
                pass_value(s + 1, h)
        for h in range(HEADS):
            pass_key(s, h)
        for h in range(HEADS):
            attend_hop(s, h)
            if s == HOPS - 1:

                @pl.when(is1)
                def _():
                    finish(h)

    @pl.when(is0)
    def _():
        for h in range(HEADS):
            attend_extra(h)
            finish(h)

    for r in range(1, n_x):
        w_shared(r).wait_recv()
    own_w.wait()
    total = dot(att[x], wfull[x], NN)
    for h in range(HEADS):
        for r in range(1, n_x):
            src = lax.rem(x + n_x - r, n_x)
            a_recv(r, h).wait_recv()
            total = total + dot(att[src, :, lanes[h]], wfull[src, lanes[h], :], NN)
    out_ref[...] = total.astype(bf16)

    exchange_d.wait_send()
    for r in range(1, n_x):
        w_send(r).wait_send()
        w_share(r).wait_send()
    for h in range(HEADS):
        for s in range(HOPS):
            v_hop(s, h).wait_send()
            k_hop(s, h).wait_send()
            v_share(s, h).wait_send()
            k_share(s, h).wait_send()
        v_extra(h, v_ref, partner).wait_send()
        k_extra(h, k_tail, partner).wait_send()
        for r in range(1, n_x):
            a_send(r, h).wait_send()


def solution(mesh):
    n_ctx = mesh.shape["ctx"]

    def body(queries, keys, values, directions, rates, selected, out_weight):
        tokens, width = queries.shape
        shard = (tokens, width)
        dma = pltpu.SemaphoreType.DMA
        vmem = pl.BlockSpec(memory_space=pltpu.VMEM)
        scratch = [
            pltpu.VMEM((HOPS,) + shard, bf16),
            pltpu.VMEM((HOPS,) + shard, bf16),
            pltpu.VMEM(shard, bf16),
            pltpu.VMEM((HOPS,) + shard, bf16),
            pltpu.VMEM((HOPS,) + shard, bf16),
            pltpu.VMEM(shard, bf16),
            pltpu.VMEM((HOPS + 1,) + shard, bf16),
            pltpu.VMEM(shard, bf16),
            pltpu.VMEM((HD, width), f32),
            pltpu.VMEM((HD, width), f32),
            pltpu.VMEM(shard, bf16),
            pltpu.VMEM(shard, bf16),
            pltpu.VMEM((HEADS, tokens, HD), f32),
            pltpu.VMEM((HEADS, tokens, HD), f32),
            pltpu.VMEM((HEADS, tokens, HD), f32),
            pltpu.VMEM((HEADS, tokens, tokens), f32),
            pltpu.VMEM((4,) + shard, bf16),
            pltpu.VMEM((4, width, width), bf16),
        ]
        hop, one = (HOPS, HEADS), (HEADS,)
        sems = [hop, hop, hop, hop, one, one] * 2 + [(), (), (3,), (3,), (3,), (3,), (3, HEADS), (3, HEADS), ()]
        scratch += [dma(s) if s else dma for s in sems]
        return pl.pallas_call(
            functools.partial(kernel, n_ctx),
            out_shape=jax.ShapeDtypeStruct(shard, bf16),
            in_specs=[
                pl.BlockSpec(memory_space=pltpu.SMEM),
                vmem, vmem, vmem, vmem, vmem,
                pl.BlockSpec(memory_space=pl.ANY),
            ],
            out_specs=vmem,
            scratch_shapes=scratch,
            compiler_params=pltpu.CompilerParams(
                collective_id=0, has_side_effects=True, vmem_limit_bytes=56 << 20
            ),
            name="path_attention",
        )(selected, queries, keys, values, directions, rates, out_weight)

    in_specs = (
        P("ctx", "head"),
        P("ctx", "head"),
        P("ctx", "head"),
        P("ctx", "head"),
        P("head", "ctx"),
        P("ctx", None),
        P("head", None),
    )
    return jax.shard_map(
        body, mesh=mesh, in_specs=in_specs, out_specs=P("ctx", "head"), check_vma=False
    )
```

time: 246 us -> 71.8 us (0.29)
  the two profiles are of different devices: /device:TPU:8 before, /device:TPU:1 now
where the time goes in v1:
time: 71.8 us; the launch traced here: 71.7 us
  Pallas kernels  70 us (97%)
  local copies, waits for them, and re-layouts  1.67 us (2%)
    pallas_call x1, Pallas kernels, body(): pl.pallas_call(functools.partial(kernel, n_ctx), out_shape=jax.ShapeDtype...  70 us
    unnamed x1, local copies, waits for them, and re-layouts  1.67 us

profile of v1, /device:TPU:1, one launch (start us, length us, event | category | flops | bytes accessed | tf_op | source)
XLA Modules:
  0.0 71.7 jit_solution(10368115670012501193)
XLA Ops:
  0.0 70.0 %path_attention.1 = bf16[256,512]{1,0:T(8,128)(2,1)} custom-call(s32[2,4]{1,0:T(2,128)} %sel.1, bf16[256,512]{1,0:T(8,128)(2,1)} %q_ref.1, bf16[256,512]{1,0:T(8,128)(2,1)} %k_ref.1, bf16[256,512]{1,0:T(8,128)(2,1)} %v_ref.1, bf16[256,512]{1,0:T(8,128)(2,1)} %w_ref.1, f32[4,256]{1,0:T(4,128)} %rate_ref.1, bf16[512,2048]{1,0:T(8,128)(2,1)} %ow_ref.1), custom_call_target="tpu_custom_call" | custom-call | tf_op jit(solution)/shard_map/path_attention/pallas_call | solution.py:435
  70.0 1.7 %copy.9 = bf16[256,512]{1,0:T(8,128)(2,1)} copy(bf16[256,512]{1,0:T(8,128)(2,1)} %path_attention.1) | data formatting | bytes 524288

commit v2 on v1

v2 whole, which is shorter than its diff:
```python
import functools

import jax
import jax.numpy as jnp
from jax import lax
from jax.experimental import pallas as pl
from jax.experimental.pallas import tpu as pltpu
from jax.sharding import PartitionSpec as P

MESH = pl.DeviceIdType.MESH
HD = 128
B = 128
HEADS = 4
NEG = -1e30
SCALE = HD ** (-0.5)
f32 = jnp.float32
bf16 = jnp.bfloat16
NN = (((1,), (0,)), ((), ()))
NT = (((1,), (1,)), ((), ()))
TN = (((0,), (0,)), ((), ()))


def dot(a, b, dims):
    return lax.dot_general(a, b, dims, preferred_element_type=f32)


def split(a):
    high = a.astype(bf16)
    return high, (a - high.astype(f32)).astype(bf16)


def dot3(a, b, dims):
    return dot(a[0], b[0], dims) + (dot(a[1], b[0], dims) + dot(a[0], b[1], dims))


def dot_left(a, b, dims):
    return dot(a[0], b, dims) + dot(a[1], b, dims)


def dot_right(a, b, dims):
    return dot(a, b[0], dims) + dot(a, b[1], dims)


def block_terms(q, k, w, beta):
    each = range(len(q))
    row = lax.broadcasted_iota(jnp.int32, (B, B), 0)
    col = lax.broadcasted_iota(jnp.int32, (B, B), 1)
    eye = (row == col).astype(f32)
    grams = [
        dot(jnp.concatenate([w[i], q[i]], 0), jnp.concatenate([w[i], k[i]], 0), NT) for i in each
    ]
    wide = [w[i].astype(f32) for i in each]
    norm = [jnp.sum(wide[i] * wide[i], -1, keepdims=True) for i in each]
    rate = [
        jnp.transpose(jnp.broadcast_to(beta[i], (B, B))) / (norm[i] + 1e-6) for i in each
    ]
    lower = [jnp.where(row > col, rate[i] * grams[i][:B, :B], 0.0) for i in each]
    key_proj = [split(jnp.where(row > col, grams[i][:B, B:], 0.0)) for i in each]
    query_proj = [split(jnp.where(row >= col, grams[i][B:, :B], 0.0)) for i in each]

    def off_diagonal(size):
        return ((row ^ col) < 2 * size) & ((row & size) != 0) & ((col & size) == 0)

    inverse = [eye - jnp.where(off_diagonal(1), lower[i], 0.0) for i in each]
    size = 2
    while size < B:
        mask = off_diagonal(size)
        parts = [split(inverse[i]) for i in each]
        below = [split(jnp.where(mask, lower[i], 0.0)) for i in each]
        step = [split(dot3(below[i], parts[i], NN)) for i in each]
        inverse = [inverse[i] - dot3(parts[i], step[i], NN) for i in each]
        size *= 2
    mixing = [split(inverse[i] * jnp.transpose(rate[i])) for i in each]
    mix_w = [split(dot_left(mixing[i], w[i], NN)) for i in each]
    mix_k = [split(dot3(mixing[i], key_proj[i], NN)) for i in each]
    block_map = [eye - dot_right(w[i], mix_w[i], TN) for i in each]
    k_end = [k[i].astype(f32) - dot_left(mix_k[i], w[i], TN) for i in each]
    q_start = [q[i].astype(f32) - dot3(query_proj[i], mix_w[i], NN) for i in each]
    inner = [grams[i][B:, B:] - dot3(query_proj[i], mix_k[i], NN) for i in each]
    return q_start, k_end, inner, block_map


def kernel(
    n_ctx, sel, q_ref, k_ref, v_ref, w_ref, rate_ref, ow_ref, out_ref,
    k_own, k_par, k_ext, v_own, v_par, v_ext, k_stage, k_tail, d_mine, d_part,
    q_front, q_home, q_in, q_vis, b_mine, b_in, o_out, o_in, s_out, s_in,
    m_ref, l_ref, acc_ref, local, att, wfull,
    sv, rv, svp, rvp, sve, rve, sk, rk, skp, rkp, ske, rke, sd, rd, sq, rq, sb, rb, so, ro, ss, rs,
    sw, rw, swp, rwp, sa, ra, sar, rar, lw,
):
    me = lax.axis_index("ctx")
    x = lax.axis_index("head")
    core = lax.rem(me, 2)
    is0 = core == 0
    is1 = core == 1
    n_x = 4
    nxt = lax.rem(me + 2, n_ctx)
    prv = lax.rem(me + n_ctx - 2, n_ctx)
    partner = me + 1 - 2 * core
    cross = jnp.where(is0, lax.rem(me + n_ctx - 1, n_ctx), lax.rem(me + 1, n_ctx))
    x_right = lax.rem(x + 1, n_x)
    x_left = lax.rem(x + n_x - 1, n_x)
    x_far = lax.rem(x + 2, n_x)
    has_next = me + 2 < n_ctx
    has_next2 = me + 4 < n_ctx
    has_prev = me >= 2
    has_prev2 = me >= 4
    crossed = (is0 & has_prev) | (is1 & has_next)
    feeds = is1 & has_prev & (me + 6 < n_ctx)
    visit1 = has_prev & has_next
    visit2 = has_prev & has_next2
    lanes = [slice(h * HD, (h + 1) * HD) for h in range(HEADS)]
    rows = [slice(n * B, (n + 1) * B) for n in range(2)]

    def remote(src, dst, send, recv, to):
        return pltpu.make_async_remote_copy(
            src_ref=src, dst_ref=dst, send_sem=send, recv_sem=recv, device_id=to, device_id_type=MESH
        )

    barrier = pltpu.get_barrier_semaphore()
    for other, there in ((nxt, has_next), (prv, has_prev), (cross, crossed)):

        @pl.when(there)
        def _():
            pl.semaphore_signal(barrier, inc=1, device_id=(other, x), device_id_type=MESH)

    pl.semaphore_signal(barrier, inc=1, device_id=(partner, x), device_id_type=MESH)
    for other in (x_right, x_far, x_left):
        pl.semaphore_signal(barrier, inc=1, device_id=(me, other), device_id_type=MESH)
    count = lambda flag: jnp.where(flag, 1, 0)
    pl.semaphore_wait(barrier, 4 + count(has_next) + count(has_prev) + count(crossed))

    def v_hop(h):
        return remote(v_ref.at[:, lanes[h]], v_own.at[:, lanes[h]], sv.at[h], rv.at[h], (nxt, x))

    def k_hop(h):
        return remote(
            k_stage.at[0, :, lanes[h]], k_own.at[:, lanes[h]], sk.at[h], rk.at[h], (nxt, x)
        )

    def v_share(h):
        return remote(
            v_own.at[:, lanes[h]], v_par.at[:, lanes[h]], svp.at[h], rvp.at[h], (partner, x)
        )

    def k_share(h):
        return remote(
            k_own.at[:, lanes[h]], k_par.at[:, lanes[h]], skp.at[h], rkp.at[h], (partner, x)
        )

    def v_extra(h, src, to):
        return remote(src.at[:, lanes[h]], v_ext.at[:, lanes[h]], sve.at[h], rve.at[h], (to, x))

    def k_extra(h, src, to):
        return remote(src.at[:, lanes[h]], k_ext.at[:, lanes[h]], ske.at[h], rke.at[h], (to, x))

    def q_hop(s, h):
        src = q_home.at[:, lanes[h]] if s == 0 else q_vis.at[0, :, lanes[h]]
        return remote(src, q_in.at[s, :, lanes[h]], sq.at[s, h], rq.at[s, h], (prv, x))

    def b_hop(s):
        src = b_mine if s == 0 else b_in.at[0]
        return remote(src, b_in.at[s], sb.at[s], rb.at[s], (prv, x))

    def o_hop(s, h):
        return remote(
            o_out.at[s, :, lanes[h]], o_in.at[s, :, lanes[h]], so.at[s, h], ro.at[s, h], (nxt, x)
        )

    def s_hop(s, h):
        return remote(s_out.at[s, h], s_in.at[s, h], ss.at[s, h], rs.at[s, h], (nxt, x))

    half = pl.ds(pl.multiple_of(core * 256, 256), 256)
    other_half = pl.ds(pl.multiple_of((1 - core) * 256, 256), 256)
    peers = [(x_right, x_left), (x_far, x_far), (x_left, x_right)]

    def w_send(r):
        to = peers[r][0]
        cols = pl.ds(pl.multiple_of(to * 512, 512), 512)
        return remote(ow_ref.at[half, cols], wfull.at[x, half], sw.at[r], rw.at[r], (me, to))

    def w_recv(r):
        src = peers[r][1]
        return remote(wfull.at[src, half], wfull.at[src, half], sw.at[r], rw.at[r], (me, src))

    def w_share(r, part):
        slot = wfull.at[peers[r][1], part]
        return remote(slot, slot, swp.at[r], rwp.at[r], (partner, x))

    def a_hop(r, h, owner, to):
        slot = att.at[owner, :, lanes[h]]
        return remote(slot, slot, sa.at[r, h], ra.at[r, h], (me, to))

    def a_relay(r, h, owner, to):
        slot = att.at[owner, rows[r], lanes[h]]
        return remote(slot, slot, sar.at[r, h], rar.at[r, h], (me, to))

    own_w = pltpu.make_async_copy(
        ow_ref.at[:, pl.ds(pl.multiple_of(x * 512, 512), 512)], wfull.at[x], lw
    )

    @pl.when(has_next)
    def _():
        for h in range(HEADS):
            v_hop(h).start()

    @pl.when(is0)
    def _():
        for h in range(HEADS):
            v_extra(h, v_ref, partner).start()

    for r in range(3):
        w_send(r).start()
    own_w.start()

    def bias(n, block):
        hit = sel[n, 0] == block
        for e in range(1, 4):
            hit = hit | (sel[n, e] == block)
        return jnp.where(hit, 0.0, NEG).astype(f32)

    away = [me - 4, me - 3 - 2 * core, me - 6, me - 5 - 2 * core, me - 7]
    for n in range(2):
        for i, device in enumerate(away):
            for b in range(2):
                line = 10 * n + 2 * i + b
                b_mine[line : line + 1, :] = jnp.full((1, HD), bias(n, 2 * device + b), f32)

    @pl.when(has_prev2)
    def _():
        b_hop(0).start()

    pairs = [(n, h) for h in range(HEADS) for n in range(2)]

    def cut(ref):
        return [ref[rows[n], lanes[h]] for n, h in pairs]

    q_start, k_end, inner, block_map = block_terms(
        cut(q_ref), cut(k_ref), cut(w_ref), [rate_ref[h : h + 1, rows[n]] for n, h in pairs]
    )
    maps = [split(m) for m in block_map]
    tails, fronts = [], []
    for h in range(HEADS):
        d_mine[:, lanes[h]] = dot3(maps[2 * h + 1], maps[2 * h], NN)
    exchange_d = remote(d_mine, d_part, sd, rd, (partner, x))
    exchange_d.start()
    for h in range(HEADS):
        first, second = 2 * h, 2 * h + 1
        early = split(k_end[first])
        tails.append(jnp.concatenate([dot3(early, maps[second], NT), k_end[second]], 0))
        late = split(q_start[second])
        fronts.append(jnp.concatenate([q_start[first], dot3(late, maps[first], NN)], 0))
        q_front[:, lanes[h]] = (fronts[h] * SCALE).astype(bf16)
        k_tail[:, lanes[h]] = tails[h].astype(bf16)
        local[h, B:, :B] = dot3(late, early, NT) * SCALE
        local[h, :B, :B] = inner[first] * SCALE
        local[h, B:, B:] = inner[second] * SCALE

    @pl.when(is0)
    def _():
        for h in range(HEADS):
            k_extra(h, k_tail, partner).start()

    @pl.when(has_prev)
    def _():
        for h in range(HEADS):
            v_hop(h).wait_recv()
            v_share(h).start()

            @pl.when(feeds)
            def _():
                v_extra(h, v_own, cross).start()

    exchange_d.wait_recv()
    chip_maps = []
    for h in range(HEADS):
        d_own = d_mine[:, lanes[h]]
        d_other = d_part[:, lanes[h]]
        other = split(d_other)
        carried = dot3(split(tails[h]), other, NT)
        k_stage[0, :, lanes[h]] = jnp.where(is0, carried, tails[h]).astype(bf16)
        moved = dot3(split(fronts[h]), other, NN)
        q_home[:, lanes[h]] = (jnp.where(is0, fronts[h], moved) * SCALE).astype(bf16)

        @pl.when(has_next)
        def _():
            k_hop(h).start()

        @pl.when(has_prev2)
        def _():
            q_hop(0, h).start()

        later = jnp.where(is0, d_other, d_own)
        sooner = jnp.where(is0, d_own, d_other)
        chip_maps.append(split(dot3(split(later), split(sooner), NN)))

    def first_block(h):
        row = lax.broadcasted_iota(jnp.int32, (B, B), 0)
        col = lax.broadcasted_iota(jnp.int32, (B, B), 1)
        for n in range(2):
            tiles = [local[h, rows[n], rows[b]] + bias(n, 2 * me + b) for b in range(n)]
            tiles.append(
                jnp.where(row >= col, local[h, rows[n], rows[n]] + bias(n, 2 * me + n), NEG)
            )
            top = functools.reduce(jnp.maximum, tiles)
            top = jnp.broadcast_to(jnp.max(top, -1, keepdims=True), (B, B))
            expos = [jnp.exp(t - top) for t in tiles]
            m_ref[h, rows[n], :] = top
            l_ref[h, rows[n], :] = functools.reduce(jnp.add, expos)
            total = jnp.zeros((B, HD), f32)
            for b, e in enumerate(expos):
                total = total + dot(e.astype(bf16), v_ref[rows[b], lanes[h]], NN)
            acc_ref[h, rows[n], :] = total

    def attend(g, query, sources, fresh=False):
        scores = [dot(query, keys, NT) for keys, _, _ in sources]
        for n in range(2):
            tiles = [
                scores[i][rows[n], rows[b]] + offset(n, b)
                for i, (_, _, offset) in enumerate(sources)
                for b in range(2)
            ]
            top = functools.reduce(jnp.maximum, tiles)
            top = jnp.broadcast_to(jnp.max(top, -1, keepdims=True), (B, B))
            if not fresh:
                old = m_ref[g, rows[n], :]
                top = jnp.maximum(old, top)
                fade = jnp.exp(old - top)
            expos = [jnp.exp(t - top) for t in tiles]
            norm = functools.reduce(jnp.add, expos)
            if not fresh:
                norm = norm + l_ref[g, rows[n], :] * fade
            m_ref[g, rows[n], :] = top
            l_ref[g, rows[n], :] = norm
            total = None if fresh else acc_ref[g, rows[n], :] * fade
            for i, (_, values, _) in enumerate(sources):
                weights = jnp.concatenate(expos[2 * i : 2 * i + 2], 1).astype(bf16)
                part = dot(weights, values, NN)
                total = part if total is None else total + part
            acc_ref[g, rows[n], :] = total

    def at_home(device):
        return lambda n, b: bias(n, 2 * device + b)

    def sent_along(s, i):
        def offset(n, b):
            line = 10 * n + 2 * i + b
            return b_in[s, line : line + 1, :]

        return offset

    def shards(h, own, other):
        return [
            (k_own[:, lanes[h]], v_own[:, lanes[h]], own),
            (k_par[:, lanes[h]], v_par[:, lanes[h]], other),
        ]

    def wait_extra(h):
        v_extra(h, v_own, cross).wait_recv()
        k_extra(h, k_tail, cross).wait_recv()

    def result(g):
        parts, logs = [], []
        for n in range(2):
            norm = jnp.sum(l_ref[g, rows[n], :], -1, keepdims=True)
            parts.append(acc_ref[g, rows[n], :] / norm)
            logs.append(jnp.transpose(m_ref[g, rows[n], :] + jnp.log(norm))[:1, :])
        return parts, logs

    def give(s, h):
        parts, logs = result((s + 1) * HEADS + h)
        for n in range(2):
            o_out[s, rows[n], lanes[h]] = parts[n].astype(bf16)
            s_out[s, h, n : n + 1, :] = logs[n]
        o_hop(s, h).start()
        s_hop(s, h).start()

    def take(s, h):
        o_hop(s, h).wait_recv()
        s_hop(s, h).wait_recv()
        g = s * HEADS + h
        for n in range(2):
            log = jnp.transpose(jnp.broadcast_to(s_in[s, h, n : n + 1, :], (B, B)))
            old = m_ref[g, rows[n], :]
            top = jnp.maximum(old, log)
            fade, weight = jnp.exp(old - top), jnp.exp(log - top)
            m_ref[g, rows[n], :] = top
            l_ref[g, rows[n], :] = l_ref[g, rows[n], :] * fade + weight * (1.0 / B)
            acc_ref[g, rows[n], :] = (
                acc_ref[g, rows[n], :] * fade + o_in[s, rows[n], lanes[h]].astype(f32) * weight
            )

    for h in range(HEADS):
        first_block(h)

    @pl.when(is1)
    def _():
        for h in range(HEADS):
            wait_extra(h)
            attend(h, q_front[:, lanes[h]], [(k_ext[:, lanes[h]], v_ext[:, lanes[h]], at_home(me - 1))])

    @pl.when(visit1)
    def _():
        b_hop(0).wait_recv()

        @pl.when(has_prev2)
        def _():
            b_hop(1).start()

    def wait_share(h):
        v_share(h).wait_recv()
        k_share(h).wait_recv()

    def near(h):
        device = me - 2
        attend(
            h,
            q_home[:, lanes[h]],
            shards(h, at_home(device), at_home(device + 1 - 2 * core)),
        )

        @pl.when(visit1)
        def _():
            attend(
                HEADS + h,
                q_vis[0, :, lanes[h]],
                shards(h, sent_along(0, 0), sent_along(0, 1)),
                fresh=True,
            )

    @pl.when(has_prev)
    def _():
        for h in range(HEADS):
            k_hop(h).wait_recv()
            k_share(h).start()

            @pl.when(feeds)
            def _():
                moved = dot_right(k_own[:, lanes[h]], chip_maps[h], NT)
                k_stage[1, :, lanes[h]] = moved.astype(bf16)
                k_extra(h, k_stage.at[1], cross).start()

            @pl.when(visit1)
            def _():
                q_hop(0, h).wait_recv()
                moved = dot_right(q_in[0, :, lanes[h]], chip_maps[h], NN)
                q_vis[0, :, lanes[h]] = moved.astype(bf16)

                @pl.when(has_prev2)
                def _():
                    q_hop(1, h).start()

            if h > 0:
                wait_share(h - 1)
                near(h - 1)
        wait_share(HEADS - 1)

    @pl.when(visit2)
    def _():
        b_hop(1).wait_recv()
        for h in range(HEADS):
            q_hop(1, h).wait_recv()
            moved = dot_right(q_in[1, :, lanes[h]], chip_maps[h], NN)
            q_vis[1, :, lanes[h]] = moved.astype(bf16)
            g = 2 * HEADS + h
            attend(
                g,
                q_vis[1, :, lanes[h]],
                shards(h, sent_along(1, 2), sent_along(1, 3)),
                fresh=True,
            )

            @pl.when(is0 & has_prev2)
            def _():
                wait_extra(h)
                attend(
                    g,
                    q_vis[1, :, lanes[h]],
                    [(k_ext[:, lanes[h]], v_ext[:, lanes[h]], sent_along(1, 4))],
                )

            give(1, h)

    for r in range(3):
        w_recv(r).wait_recv()
        w_share(r, half).start()

    @pl.when(has_prev)
    def _():
        near(HEADS - 1)

    @pl.when(visit1)
    def _():
        for h in range(HEADS):

            @pl.when(has_prev2)
            def _():
                take(1, h)

            give(0, h)

    def pass_head(h):
        a_hop(0, h, x_left, x_left).wait_recv()
        a_relay(0, h, x_left, x_right).start()
        a_hop(1, h, x_right, x_right).wait_recv()
        a_relay(1, h, x_right, x_left).start()

    for h in range(HEADS):

        @pl.when(has_prev2)
        def _():
            take(0, h)

        parts, _ = result(h)
        for n in range(2):
            att[x, rows[n], lanes[h]] = parts[n].astype(bf16)
        a_hop(0, h, x, x_right).start()
        a_hop(1, h, x, x_left).start()
        if h > 0:
            pass_head(h - 1)

    for r in range(3):
        w_share(r, other_half).wait_recv()
    own_w.wait()
    total = dot(att[x], wfull[x], NN)
    for h in range(HEADS):
        if h == HEADS - 1:
            pass_head(h)
        for src in (x_left, x_right):
            total = total + dot(att[src, :, lanes[h]], wfull[src, lanes[h], :], NN)
    for h in range(HEADS):
        a_relay(0, h, x_far, x_left).wait_recv()
        a_relay(1, h, x_far, x_right).wait_recv()
        total = total + dot(att[x_far, :, lanes[h]], wfull[x_far, lanes[h], :], NN)
    out_ref[...] = total.astype(bf16)

    exchange_d.wait_send()
    for r in range(3):
        w_send(r).wait_send()
        w_share(r, half).wait_send()
    for h in range(HEADS):
        a_hop(0, h, x, x_right).wait_send()
        a_hop(1, h, x, x_left).wait_send()
        a_relay(0, h, x_left, x_right).wait_send()
        a_relay(1, h, x_right, x_left).wait_send()

    @pl.when(has_next)
    def _():
        for h in range(HEADS):
            v_hop(h).wait_send()
            k_hop(h).wait_send()

    @pl.when(has_prev)
    def _():
        for h in range(HEADS):
            v_share(h).wait_send()
            k_share(h).wait_send()

    @pl.when(is0 | feeds)
    def _():
        for h in range(HEADS):
            v_extra(h, v_own, cross).wait_send()
            k_extra(h, k_tail, cross).wait_send()

    @pl.when(has_prev2)
    def _():
        b_hop(0).wait_send()
        for h in range(HEADS):
            q_hop(0, h).wait_send()

    @pl.when(visit1 & has_prev2)
    def _():
        b_hop(1).wait_send()
        for h in range(HEADS):
            q_hop(1, h).wait_send()

    for s, given in ((0, visit1), (1, visit2)):

        @pl.when(given)
        def _():
            for h in range(HEADS):
                o_hop(s, h).wait_send()
                s_hop(s, h).wait_send()


def solution(mesh):
    n_ctx = mesh.shape["ctx"]

    def body(queries, keys, values, directions, rates, selected, out_weight):
        tokens, width = queries.shape
        shard = (tokens, width)
        dma = pltpu.SemaphoreType.DMA
        vmem = pl.BlockSpec(memory_space=pltpu.VMEM)
        slab = pltpu.VMEM(shard, bf16)
        square = pltpu.VMEM((HD, width), f32)
        state = pltpu.VMEM((3 * HEADS, tokens, HD), f32)

        def pair(shape, dtype):
            return pltpu.VMEM((2,) + shape, dtype)

        scratch = [slab] * 6 + [pair(shard, bf16), slab, square, square]
        scratch += [slab, slab, pair(shard, bf16), pair(shard, bf16)]
        scratch += [pltpu.VMEM((20, HD), f32), pair((20, HD), f32)]
        scratch += [pair(shard, bf16), pair(shard, bf16)]
        scratch += [pair((HEADS, 2, HD), f32), pair((HEADS, 2, HD), f32)]
        scratch += [state, state, state, pltpu.VMEM((HEADS, tokens, tokens), f32)]
        scratch += [pltpu.VMEM((4,) + shard, bf16), pltpu.VMEM((4, width, width), bf16)]
        each, two = (HEADS,), (2, HEADS)
        sems = [each] * 12 + [(), (), two, two, (2,), (2,), two, two, two, two]
        sems += [(3,), (3,), (3,), (3,), two, two, two, two, ()]
        scratch += [dma(s) if s else dma for s in sems]
        return pl.pallas_call(
            functools.partial(kernel, n_ctx),
            out_shape=jax.ShapeDtypeStruct(shard, bf16),
            in_specs=[
                pl.BlockSpec(memory_space=pltpu.SMEM),
                vmem, vmem, vmem, vmem, vmem,
                pl.BlockSpec(memory_space=pl.ANY),
            ],
            out_specs=vmem,
            scratch_shapes=scratch,
            compiler_params=pltpu.CompilerParams(
                collective_id=0, has_side_effects=True, vmem_limit_bytes=56 << 20
            ),
            name="path_attention",
        )(selected, queries, keys, values, directions, rates, out_weight)

    in_specs = (
        P("ctx", "head"),
        P("ctx", "head"),
        P("ctx", "head"),
        P("ctx", "head"),
        P("head", "ctx"),
        P("ctx", None),
        P("head", None),
    )
    return jax.shard_map(
        body, mesh=mesh, in_specs=in_specs, out_specs=P("ctx", "head"), check_vma=False
    )
```

time: 71.8 us -> 55.9 us (0.78)
  the two profiles are of different devices: /device:TPU:1 before, /device:TPU:256 now
where the time goes in v2:
time: 55.9 us; the launch traced here: 55.7 us
  Pallas kernels  54 us (97%)
  local copies, waits for them, and re-layouts  1.67 us (3%)
    pallas_call x1, Pallas kernels, body(): pl.pallas_call(functools.partial(kernel, n_ctx), out_shape=jax.ShapeDtype...  54 us
    unnamed x1, local copies, waits for them, and re-layouts  1.67 us

profile of v2, /device:TPU:256, one launch (start us, length us, event | category | flops | bytes accessed | tf_op | source)
XLA Modules:
  0.0 55.7 jit_solution(6985064783349122602)
XLA Ops:
  0.0 54.0 %path_attention.1 = bf16[256,512]{1,0:T(8,128)(2,1)} custom-call(s32[2,4]{1,0:T(2,128)} %sel.1, bf16[256,512]{1,0:T(8,128)(2,1)} %q_ref.1, bf16[256,512]{1,0:T(8,128)(2,1)} %k_ref.1, bf16[256,512]{1,0:T(8,128)(2,1)} %v_ref.1, bf16[256,512]{1,0:T(8,128)(2,1)} %w_ref.1, f32[4,256]{1,0:T(4,128)} %rate_ref.1, bf16[512,2048]{1,0:T(8,128)(2,1)} %ow_ref.1), custom_call_target="tpu_custom_call" | custom-call | tf_op jit(solution)/shard_map/path_attention/pallas_call | solution.py:612
  54.1 1.7 %copy.9 = bf16[256,512]{1,0:T(8,128)(2,1)} copy(bf16[256,512]{1,0:T(8,128)(2,1)} %path_attention.1) | data formatting | bytes 524288

commit v3 on v2

--- a/solution.py
+++ b/solution.py
@@ -12,6 +12,7 @@
 B = 128
 HEADS = 4
 NEG = -1e30
+PAUSE_AT = 4
 SCALE = HD ** (-0.5)
 f32 = jnp.float32
 bf16 = jnp.bfloat16
@@ -41,7 +42,7 @@
     return dot(a, b[0], dims) + dot(a, b[1], dims)
 
 
-def block_terms(q, k, w, beta):
+def block_terms(q, k, w, beta, pause, pause_at):
     each = range(len(q))
     row = lax.broadcasted_iota(jnp.int32, (B, B), 0)
     col = lax.broadcasted_iota(jnp.int32, (B, B), 1)
@@ -69,6 +70,8 @@
         below = [split(jnp.where(mask, lower[i], 0.0)) for i in each]
         step = [split(dot3(below[i], parts[i], NN)) for i in each]
         inverse = [inverse[i] - dot3(parts[i], step[i], NN) for i in each]
+        if size == pause_at:
+            pause()
         size *= 2
     mixing = [split(inverse[i] * jnp.transpose(rate[i])) for i in each]
     mix_w = [split(dot_left(mixing[i], w[i], NN)) for i in each]
@@ -81,12 +84,13 @@
 
 
 def kernel(
-    n_ctx, sel, q_ref, k_ref, v_ref, w_ref, rate_ref, ow_ref, out_ref,
+    n_ctx, sel, q_hbm, k_hbm, v_hbm, w_hbm, rate_hbm, ow_ref, out_ref,
+    q_ref, k_ref, v_ref, w_ref, rate_ref,
     k_own, k_par, k_ext, v_own, v_par, v_ext, k_stage, k_tail, d_mine, d_part,
     q_front, q_home, q_in, q_vis, b_mine, b_in, o_out, o_in, s_out, s_in,
     m_ref, l_ref, acc_ref, local, att, wfull,
     sv, rv, svp, rvp, sve, rve, sk, rk, skp, rkp, ske, rke, sd, rd, sq, rq, sb, rb, so, ro, ss, rs,
-    sw, rw, swp, rwp, sa, ra, sar, rar, lw,
+    sw, rw, swp, rwp, sa, ra, sar, rar, lw, li,
 ):
     me = lax.axis_index("ctx")
     x = lax.axis_index("head")
@@ -128,10 +132,18 @@
     for other in (x_right, x_far, x_left):
         pl.semaphore_signal(barrier, inc=1, device_id=(me, other), device_id_type=MESH)
     count = lambda flag: jnp.where(flag, 1, 0)
-    pl.semaphore_wait(barrier, 4 + count(has_next) + count(has_prev) + count(crossed))
+    greetings = 4 + count(has_next) + count(has_prev) + count(crossed)
+    inputs = [
+        pltpu.make_async_copy(source, target, li.at[i])
+        for i, (source, target) in enumerate(
+            ((w_hbm, w_ref), (k_hbm, k_ref), (q_hbm, q_ref), (rate_hbm, rate_ref), (v_hbm, v_ref))
+        )
+    ]
+    for copy in inputs:
+        copy.start()
 
     def v_hop(h):
-        return remote(v_ref.at[:, lanes[h]], v_own.at[:, lanes[h]], sv.at[h], rv.at[h], (nxt, x))
+        return remote(v_hbm.at[:, lanes[h]], v_own.at[:, lanes[h]], sv.at[h], rv.at[h], (nxt, x))
 
     def k_hop(h):
         return remote(
@@ -199,19 +211,26 @@
         ow_ref.at[:, pl.ds(pl.multiple_of(x * 512, 512), 512)], wfull.at[x], lw
     )
 
-    @pl.when(has_next)
-    def _():
-        for h in range(HEADS):
-            v_hop(h).start()
-
-    @pl.when(is0)
-    def _():
-        for h in range(HEADS):
-            v_extra(h, v_ref, partner).start()
-
-    for r in range(3):
-        w_send(r).start()
-    own_w.start()
+    def leave():
+        pl.semaphore_wait(barrier, greetings)
+
+        @pl.when(has_next)
+        def _():
+            for h in range(HEADS):
+                v_hop(h).start()
+
+        @pl.when(is0)
+        def _():
+            for h in range(HEADS):
+                v_extra(h, v_hbm, partner).start()
+
+        for r in range(3):
+            w_send(r).start()
+        own_w.start()
+
+        @pl.when(has_prev2)
+        def _():
+            b_hop(0).start()
 
     def bias(n, block):
         hit = sel[n, 0] == block
@@ -219,24 +238,28 @@
             hit = hit | (sel[n, e] == block)
         return jnp.where(hit, 0.0, NEG).astype(f32)
 
-    away = [me - 4, me - 3 - 2 * core, me - 6, me - 5 - 2 * core, me - 7]
+    away = [me - 4, me - 3 - 2 * core, me - 6, me - 5 - 2 * core, jnp.where(is0, me - 7, -1)]
     for n in range(2):
         for i, device in enumerate(away):
             for b in range(2):
                 line = 10 * n + 2 * i + b
                 b_mine[line : line + 1, :] = jnp.full((1, HD), bias(n, 2 * device + b), f32)
 
-    @pl.when(has_prev2)
-    def _():
-        b_hop(0).start()
+    @pl.when(is0 & (me < 4))
+    def _():
+        k_ext[...] = jnp.zeros_like(k_ext)
+        v_ext[...] = jnp.zeros_like(v_ext)
 
     pairs = [(n, h) for h in range(HEADS) for n in range(2)]
 
     def cut(ref):
         return [ref[rows[n], lanes[h]] for n, h in pairs]
 
+    for copy in inputs[:4]:
+        copy.wait()
     q_start, k_end, inner, block_map = block_terms(
-        cut(q_ref), cut(k_ref), cut(w_ref), [rate_ref[h : h + 1, rows[n]] for n, h in pairs]
+        cut(q_ref), cut(k_ref), cut(w_ref), [rate_ref[h : h + 1, rows[n]] for n, h in pairs],
+        leave, PAUSE_AT,
     )
     maps = [split(m) for m in block_map]
     tails, fronts = [], []
@@ -261,38 +284,42 @@
         for h in range(HEADS):
             k_extra(h, k_tail, partner).start()
 
-    @pl.when(has_prev)
-    def _():
-        for h in range(HEADS):
-            v_hop(h).wait_recv()
-            v_share(h).start()
-
-            @pl.when(feeds)
-            def _():
-                v_extra(h, v_own, cross).start()
-
+    def pass_values(heads):
+        @pl.when(has_prev)
+        def _():
+            for h in heads:
+                v_hop(h).wait_recv()
+                v_share(h).start()
+
+    pass_values((0,))
     exchange_d.wait_recv()
+    others = [split(d_part[:, lanes[h]]) for h in range(HEADS)]
+    for h in range(HEADS):
+        moved = dot3(split(fronts[h]), others[h], NN)
+        q_home[:, lanes[h]] = (jnp.where(is0, fronts[h], moved) * SCALE).astype(bf16)
+
+    @pl.when(has_prev2)
+    def _():
+        for h in range(HEADS):
+            q_hop(0, h).start()
+
+    for h in range(HEADS):
+        carried = dot3(split(tails[h]), others[h], NT)
+        k_stage[0, :, lanes[h]] = jnp.where(is0, carried, tails[h]).astype(bf16)
+
+    @pl.when(has_next)
+    def _():
+        for h in range(HEADS):
+            k_hop(h).start()
+
     chip_maps = []
     for h in range(HEADS):
         d_own = d_mine[:, lanes[h]]
         d_other = d_part[:, lanes[h]]
-        other = split(d_other)
-        carried = dot3(split(tails[h]), other, NT)
-        k_stage[0, :, lanes[h]] = jnp.where(is0, carried, tails[h]).astype(bf16)
-        moved = dot3(split(fronts[h]), other, NN)
-        q_home[:, lanes[h]] = (jnp.where(is0, fronts[h], moved) * SCALE).astype(bf16)
-
-        @pl.when(has_next)
-        def _():
-            k_hop(h).start()
-
-        @pl.when(has_prev2)
-        def _():
-            q_hop(0, h).start()
-
         later = jnp.where(is0, d_other, d_own)
         sooner = jnp.where(is0, d_own, d_other)
         chip_maps.append(split(dot3(split(later), split(sooner), NN)))
+    pass_values((1, 2, 3))
 
     def first_block(h):
         row = lax.broadcasted_iota(jnp.int32, (B, B), 0)
@@ -390,6 +417,7 @@
                 acc_ref[g, rows[n], :] * fade + o_in[s, rows[n], lanes[h]].astype(f32) * weight
             )
 
+    inputs[4].wait()
     for h in range(HEADS):
         first_block(h)
 
@@ -418,15 +446,12 @@
             q_home[:, lanes[h]],
             shards(h, at_home(device), at_home(device + 1 - 2 * core)),
         )
-
-        @pl.when(visit1)
-        def _():
-            attend(
-                HEADS + h,
-                q_vis[0, :, lanes[h]],
-                shards(h, sent_along(0, 0), sent_along(0, 1)),
-                fresh=True,
-            )
+        attend(
+            HEADS + h,
+            q_vis[0, :, lanes[h]],
+            shards(h, sent_along(0, 0), sent_along(0, 1)),
+            fresh=True,
+        )
 
     @pl.when(has_prev)
     def _():
@@ -439,6 +464,7 @@
                 moved = dot_right(k_own[:, lanes[h]], chip_maps[h], NT)
                 k_stage[1, :, lanes[h]] = moved.astype(bf16)
                 k_extra(h, k_stage.at[1], cross).start()
+                v_extra(h, v_own, cross).start()
 
             @pl.when(visit1)
             def _():
@@ -455,49 +481,54 @@
                 near(h - 1)
         wait_share(HEADS - 1)
 
-    @pl.when(visit2)
-    def _():
-        b_hop(1).wait_recv()
-        for h in range(HEADS):
+    def far(h):
+        @pl.when(visit2)
+        def _():
             q_hop(1, h).wait_recv()
             moved = dot_right(q_in[1, :, lanes[h]], chip_maps[h], NN)
             q_vis[1, :, lanes[h]] = moved.astype(bf16)
-            g = 2 * HEADS + h
-            attend(
-                g,
-                q_vis[1, :, lanes[h]],
-                shards(h, sent_along(1, 2), sent_along(1, 3)),
-                fresh=True,
-            )
 
             @pl.when(is0 & has_prev2)
             def _():
                 wait_extra(h)
-                attend(
-                    g,
-                    q_vis[1, :, lanes[h]],
-                    [(k_ext[:, lanes[h]], v_ext[:, lanes[h]], sent_along(1, 4))],
-                )
-
+
+            attend(
+                2 * HEADS + h,
+                q_vis[1, :, lanes[h]],
+                shards(h, sent_along(1, 2), sent_along(1, 3))
+                + [(k_ext[:, lanes[h]], v_ext[:, lanes[h]], sent_along(1, 4))],
+                fresh=True,
+            )
             give(1, h)
+
+    def back(h):
+        @pl.when(visit1)
+        def _():
+            @pl.when(has_prev2)
+            def _():
+                take(1, h)
+
+            give(0, h)
+
+    @pl.when(visit2)
+    def _():
+        b_hop(1).wait_recv()
+
+    far(0)
+    far(1)
+    far(2)
+
+    @pl.when(has_prev)
+    def _():
+        near(HEADS - 1)
 
     for r in range(3):
         w_recv(r).wait_recv()
         w_share(r, half).start()
-
-    @pl.when(has_prev)
-    def _():
-        near(HEADS - 1)
-
-    @pl.when(visit1)
-    def _():
-        for h in range(HEADS):
-
-            @pl.when(has_prev2)
-            def _():
-                take(1, h)
-
-            give(0, h)
+    back(0)
+    far(3)
+    back(1)
+    back(2)
 
     def pass_head(h):
         a_hop(0, h, x_left, x_left).wait_recv()
@@ -505,8 +536,7 @@
         a_hop(1, h, x_right, x_right).wait_recv()
         a_relay(1, h, x_right, x_left).start()
 
-    for h in range(HEADS):
-
+    def finish(h):
         @pl.when(has_prev2)
         def _():
             take(0, h)
@@ -516,18 +546,29 @@
             att[x, rows[n], lanes[h]] = parts[n].astype(bf16)
         a_hop(0, h, x, x_right).start()
         a_hop(1, h, x, x_left).start()
-        if h > 0:
-            pass_head(h - 1)
+
+    finish(0)
+    back(3)
+    finish(1)
+    finish(2)
+    pass_head(0)
+    finish(3)
+    pass_head(1)
 
     for r in range(3):
         w_share(r, other_half).wait_recv()
     own_w.wait()
     total = dot(att[x], wfull[x], NN)
-    for h in range(HEADS):
-        if h == HEADS - 1:
-            pass_head(h)
+
+    def near_part(total, h):
         for src in (x_left, x_right):
             total = total + dot(att[src, :, lanes[h]], wfull[src, lanes[h], :], NN)
+        return total
+
+    pass_head(2)
+    total = near_part(near_part(total, 0), 1)
+    pass_head(3)
+    total = near_part(near_part(total, 2), 3)
     for h in range(HEADS):
         a_relay(0, h, x_far, x_left).wait_recv()
         a_relay(1, h, x_far, x_right).wait_recv()
@@ -598,7 +639,8 @@
         def pair(shape, dtype):
             return pltpu.VMEM((2,) + shape, dtype)
 
-        scratch = [slab] * 6 + [pair(shard, bf16), slab, square, square]
+        scratch = [slab] * 4 + [pltpu.VMEM(rates.shape, f32)]
+        scratch += [slab] * 6 + [pair(shard, bf16), slab, square, square]
         scratch += [slab, slab, pair(shard, bf16), pair(shard, bf16)]
         scratch += [pltpu.VMEM((20, HD), f32), pair((20, HD), f32)]
         scratch += [pair(shard, bf16), pair(shard, bf16)]
@@ -607,16 +649,15 @@
         scratch += [pltpu.VMEM((4,) + shard, bf16), pltpu.VMEM((4, width, width), bf16)]
         each, two = (HEADS,), (2, HEADS)
         sems = [each] * 12 + [(), (), two, two, (2,), (2,), two, two, two, two]
-        sems += [(3,), (3,), (3,), (3,), two, two, two, two, ()]
+        sems += [(3,), (3,), (3,), (3,), two, two, two, two, (), (5,)]
         scratch += [dma(s) if s else dma for s in sems]
         return pl.pallas_call(
             functools.partial(kernel, n_ctx),
-            out_shape=jax.ShapeDtypeStruct(shard, bf16),
+            out_shape=pltpu.VMEM(shard, bf16),
             in_specs=[
                 pl.BlockSpec(memory_space=pltpu.SMEM),
-                vmem, vmem, vmem, vmem, vmem,
-                pl.BlockSpec(memory_space=pl.ANY),
-            ],
+            ]
+            + [pl.BlockSpec(memory_space=pl.ANY)] * 6,
             out_specs=vmem,
             scratch_shapes=scratch,
             compiler_params=pltpu.CompilerParams(

time: 55.9 us -> 48.8 us (0.87)
  Pallas kernels: 54 us -> 48 us
  local copies, waits for them, and re-layouts: 1.67 us -> 0.71 us
    pallas_call x1, Pallas kernels: 54 us -> 48 us  [body(): pl.pallas_call(functools.partial(kernel, n_ctx), out_shape=pltpu.VMEM(sha...]
    unnamed x1, local copies, waits for them, and re-layouts: 1.67 us -> 0.71 us
where the time goes in v3:
time: 48.8 us; the launch traced here: 48.7 us
  Pallas kernels  48 us (98%)
  local copies, waits for them, and re-layouts  0.71 us (1%)
    pallas_call x1, Pallas kernels, body(): pl.pallas_call(functools.partial(kernel, n_ctx), out_shape=pltpu.VMEM(sha...  48 us

profile of v3, /device:TPU:256, one launch (start us, length us, event | category | flops | bytes accessed | tf_op | source)
XLA Modules:
  0.0 48.7 jit_solution(9601982541211706102)
XLA Ops:
  0.0 48.0 %path_attention.1 = bf16[256,512]{1,0:T(8,128)(2,1)S(1)} custom-call(s32[2,4]{1,0:T(2,128)} %sel.1, bf16[256,512]{1,0:T(8,128)(2,1)} %q_hbm.1, bf16[256,512]{1,0:T(8,128)(2,1)} %k_hbm.1, bf16[256,512]{1,0:T(8,128)(2,1)} %v_hbm.1, bf16[256,512]{1,0:T(8,128)(2,1)} %w_hbm.1, f32[4,256]{1,0:T(4,128)} %rate_hbm.1, bf16[512,2048]{1,0:T(8,128)(2,1)} %ow_ref.1), custom_call_target="tpu_custom_call" | custom-call | tf_op jit(solution)/shard_map/path_attention/pallas_call | solution.py:654
  48.0 0.7 %copy.9 = bf16[256,512]{1,0:T(8,128)(2,1)} copy(bf16[256,512]{1,0:T(8,128)(2,1)S(1)} %path_attention.1) | data formatting | bytes 524288

commit v4 on v3

--- a/solution.py
+++ b/solution.py
@@ -84,8 +84,8 @@
 
 
 def kernel(
-    n_ctx, sel, q_hbm, k_hbm, v_hbm, w_hbm, rate_hbm, ow_ref, out_ref,
-    q_ref, k_ref, v_ref, w_ref, rate_ref,
+    n_ctx, sel_hbm, q_hbm, k_hbm, v_hbm, w_hbm, rate_hbm, ow_ref, out_ref,
+    sel, q_ref, k_ref, v_ref, w_ref, rate_ref,
     k_own, k_par, k_ext, v_own, v_par, v_ext, k_stage, k_tail, d_mine, d_part,
     q_front, q_home, q_in, q_vis, b_mine, b_in, o_out, o_in, s_out, s_in,
     m_ref, l_ref, acc_ref, local, att, wfull,
@@ -136,7 +136,10 @@
     inputs = [
         pltpu.make_async_copy(source, target, li.at[i])
         for i, (source, target) in enumerate(
-            ((w_hbm, w_ref), (k_hbm, k_ref), (q_hbm, q_ref), (rate_hbm, rate_ref), (v_hbm, v_ref))
+            (
+                (sel_hbm, sel), (w_hbm, w_ref), (k_hbm, k_ref), (q_hbm, q_ref),
+                (rate_hbm, rate_ref), (v_hbm, v_ref),
+            )
         )
     ]
     for copy in inputs:
@@ -199,9 +202,9 @@
         slot = wfull.at[peers[r][1], part]
         return remote(slot, slot, swp.at[r], rwp.at[r], (partner, x))
 
-    def a_hop(r, h, owner, to):
-        slot = att.at[owner, :, lanes[h]]
-        return remote(slot, slot, sa.at[r, h], ra.at[r, h], (me, to))
+    def a_hop(r, h, part, owner, to):
+        slot = att.at[owner, rows[part], lanes[h]]
+        return remote(slot, slot, sa.at[r, h, part], ra.at[r, h, part], (me, to))
 
     def a_relay(r, h, owner, to):
         slot = att.at[owner, rows[r], lanes[h]]
@@ -238,6 +241,7 @@
             hit = hit | (sel[n, e] == block)
         return jnp.where(hit, 0.0, NEG).astype(f32)
 
+    inputs[0].wait()
     away = [me - 4, me - 3 - 2 * core, me - 6, me - 5 - 2 * core, jnp.where(is0, me - 7, -1)]
     for n in range(2):
         for i, device in enumerate(away):
@@ -255,7 +259,7 @@
     def cut(ref):
         return [ref[rows[n], lanes[h]] for n, h in pairs]
 
-    for copy in inputs[:4]:
+    for copy in inputs[1:5]:
         copy.wait()
     q_start, k_end, inner, block_map = block_terms(
         cut(q_ref), cut(k_ref), cut(w_ref), [rate_ref[h : h + 1, rows[n]] for n, h in pairs],
@@ -417,7 +421,7 @@
                 acc_ref[g, rows[n], :] * fade + o_in[s, rows[n], lanes[h]].astype(f32) * weight
             )
 
-    inputs[4].wait()
+    inputs[5].wait()
     for h in range(HEADS):
         first_block(h)
 
@@ -531,9 +535,9 @@
     back(2)
 
     def pass_head(h):
-        a_hop(0, h, x_left, x_left).wait_recv()
+        a_hop(0, h, 0, x_left, x_left).wait_recv()
         a_relay(0, h, x_left, x_right).start()
-        a_hop(1, h, x_right, x_right).wait_recv()
+        a_hop(1, h, 1, x_right, x_right).wait_recv()
         a_relay(1, h, x_right, x_left).start()
 
     def finish(h):
@@ -544,8 +548,9 @@
         parts, _ = result(h)
         for n in range(2):
             att[x, rows[n], lanes[h]] = parts[n].astype(bf16)
-        a_hop(0, h, x, x_right).start()
-        a_hop(1, h, x, x_left).start()
+        for part in range(2):
+            a_hop(0, h, part, x, x_right).start()
+            a_hop(1, h, 1 - part, x, x_left).start()
 
     finish(0)
     back(3)
@@ -561,13 +566,15 @@
     total = dot(att[x], wfull[x], NN)
 
     def near_part(total, h):
+        a_hop(0, h, 1, x_left, x_left).wait_recv()
+        a_hop(1, h, 0, x_right, x_right).wait_recv()
         for src in (x_left, x_right):
             total = total + dot(att[src, :, lanes[h]], wfull[src, lanes[h], :], NN)
         return total
 
     pass_head(2)
+    pass_head(3)
     total = near_part(near_part(total, 0), 1)
-    pass_head(3)
     total = near_part(near_part(total, 2), 3)
     for h in range(HEADS):
         a_relay(0, h, x_far, x_left).wait_recv()
@@ -580,8 +587,9 @@
         w_send(r).wait_send()
         w_share(r, half).wait_send()
     for h in range(HEADS):
-        a_hop(0, h, x, x_right).wait_send()
-        a_hop(1, h, x, x_left).wait_send()
+        for part in range(2):
+            a_hop(0, h, part, x, x_right).wait_send()
+            a_hop(1, h, part, x, x_left).wait_send()
         a_relay(0, h, x_left, x_right).wait_send()
         a_relay(1, h, x_right, x_left).wait_send()
 
@@ -639,7 +647,7 @@
         def pair(shape, dtype):
             return pltpu.VMEM((2,) + shape, dtype)
 
-        scratch = [slab] * 4 + [pltpu.VMEM(rates.shape, f32)]
+        scratch = [pltpu.SMEM(selected.shape, jnp.int32)] + [slab] * 4 + [pltpu.VMEM(rates.shape, f32)]
         scratch += [slab] * 6 + [pair(shard, bf16), slab, square, square]
         scratch += [slab, slab, pair(shard, bf16), pair(shard, bf16)]
         scratch += [pltpu.VMEM((20, HD), f32), pair((20, HD), f32)]
@@ -647,17 +655,16 @@
         scratch += [pair((HEADS, 2, HD), f32), pair((HEADS, 2, HD), f32)]
         scratch += [state, state, state, pltpu.VMEM((HEADS, tokens, tokens), f32)]
         scratch += [pltpu.VMEM((4,) + shard, bf16), pltpu.VMEM((4, width, width), bf16)]
-        each, two = (HEADS,), (2, HEADS)
+        each, two, halves = (HEADS,), (2, HEADS), (2, HEADS, 2)
         sems = [each] * 12 + [(), (), two, two, (2,), (2,), two, two, two, two]
-        sems += [(3,), (3,), (3,), (3,), two, two, two, two, (), (5,)]
+        sems += [(3,), (3,), (3,), (3,), halves, halves, two, two, (), (6,)]
         scratch += [dma(s) if s else dma for s in sems]
         return pl.pallas_call(
             functools.partial(kernel, n_ctx),
             out_shape=pltpu.VMEM(shard, bf16),
             in_specs=[
-                pl.BlockSpec(memory_space=pltpu.SMEM),
             ]
-            + [pl.BlockSpec(memory_space=pl.ANY)] * 6,
+            + [pl.BlockSpec(memory_space=pl.ANY)] * 7,
             out_specs=vmem,
             scratch_shapes=scratch,
             compiler_params=pltpu.CompilerParams(

time: 48.8 us -> 47.8 us (0.980)
  Pallas kernels: 48 us -> 46.9 us
    pallas_call x1, Pallas kernels: 48 us -> 46.9 us  [body(): pl.pallas_call(functools.partial(kernel, n_ctx), out_shape=pltpu.VMEM(sha...]
where the time goes in v4:
time: 47.8 us; the launch traced here: 47.6 us
  Pallas kernels  46.9 us (98%)
  local copies, waits for them, and re-layouts  0.71 us (1%)
    pallas_call x1, Pallas kernels, body(): pl.pallas_call(functools.partial(kernel, n_ctx), out_shape=pltpu.VMEM(sha...  46.9 us

profile of v4, /device:TPU:256, one launch (start us, length us, event | category | flops | bytes accessed | tf_op | source)
XLA Modules:
  0.0 47.6 jit_solution(17866566461863198861)
XLA Ops:
  0.0 46.9 %path_attention.1 = bf16[256,512]{1,0:T(8,128)(2,1)S(1)} custom-call(s32[2,4]{1,0:T(2,128)} %sel_hbm.1, bf16[256,512]{1,0:T(8,128)(2,1)} %q_hbm.1, bf16[256,512]{1,0:T(8,128)(2,1)} %k_hbm.1, bf16[256,512]{1,0:T(8,128)(2,1)} %v_hbm.1, bf16[256,512]{1,0:T(8,128)(2,1)} %w_hbm.1, f32[4,256]{1,0:T(4,128)} %rate_hbm.1, bf16[512,2048]{1,0:T(8,128)(2,1)} %ow_ref.1), custom_call_target="tpu_custom_call" | custom-call | tf_op jit(solution)/shard_map/path_attention/pallas_call | solution.py:662
  46.9 0.7 %copy.9 = bf16[256,512]{1,0:T(8,128)(2,1)} copy(bf16[256,512]{1,0:T(8,128)(2,1)S(1)} %path_attention.1) | data formatting | bytes 524288

commit v5 on v4

--- a/solution.py
+++ b/solution.py
@@ -177,9 +177,10 @@
         src = b_mine if s == 0 else b_in.at[0]
         return remote(src, b_in.at[s], sb.at[s], rb.at[s], (prv, x))
 
-    def o_hop(s, h):
+    def o_hop(s, h, n):
         return remote(
-            o_out.at[s, :, lanes[h]], o_in.at[s, :, lanes[h]], so.at[s, h], ro.at[s, h], (nxt, x)
+            o_out.at[s, rows[n], lanes[h]], o_in.at[s, rows[n], lanes[h]],
+            so.at[s, h, n], ro.at[s, h, n], (nxt, x),
         )
 
     def s_hop(s, h):
@@ -403,23 +404,27 @@
         for n in range(2):
             o_out[s, rows[n], lanes[h]] = parts[n].astype(bf16)
             s_out[s, h, n : n + 1, :] = logs[n]
-        o_hop(s, h).start()
         s_hop(s, h).start()
+        for n in range(2):
+            o_hop(s, h, n).start()
+
+    def merge(s, h, n):
+        g = s * HEADS + h
+        o_hop(s, h, n).wait_recv()
+        log = jnp.transpose(jnp.broadcast_to(s_in[s, h, n : n + 1, :], (B, B)))
+        old = m_ref[g, rows[n], :]
+        top = jnp.maximum(old, log)
+        fade, weight = jnp.exp(old - top), jnp.exp(log - top)
+        m_ref[g, rows[n], :] = top
+        l_ref[g, rows[n], :] = l_ref[g, rows[n], :] * fade + weight * (1.0 / B)
+        acc_ref[g, rows[n], :] = (
+            acc_ref[g, rows[n], :] * fade + o_in[s, rows[n], lanes[h]].astype(f32) * weight
+        )
 
     def take(s, h):
-        o_hop(s, h).wait_recv()
         s_hop(s, h).wait_recv()
-        g = s * HEADS + h
         for n in range(2):
-            log = jnp.transpose(jnp.broadcast_to(s_in[s, h, n : n + 1, :], (B, B)))
-            old = m_ref[g, rows[n], :]
-            top = jnp.maximum(old, log)
-            fade, weight = jnp.exp(old - top), jnp.exp(log - top)
-            m_ref[g, rows[n], :] = top
-            l_ref[g, rows[n], :] = l_ref[g, rows[n], :] * fade + weight * (1.0 / B)
-            acc_ref[g, rows[n], :] = (
-                acc_ref[g, rows[n], :] * fade + o_in[s, rows[n], lanes[h]].astype(f32) * weight
-            )
+            merge(s, h, n)
 
     inputs[5].wait()
     for h in range(HEADS):
@@ -541,16 +546,18 @@
         a_relay(1, h, x_right, x_left).start()
 
     def finish(h):
-        @pl.when(has_prev2)
-        def _():
-            take(0, h)
-
-        parts, _ = result(h)
         for n in range(2):
-            att[x, rows[n], lanes[h]] = parts[n].astype(bf16)
-        for part in range(2):
-            a_hop(0, h, part, x, x_right).start()
-            a_hop(1, h, 1 - part, x, x_left).start()
+
+            @pl.when(has_prev2)
+            def _():
+                if n == 0:
+                    s_hop(0, h).wait_recv()
+                merge(0, h, n)
+
+            norm = jnp.sum(l_ref[h, rows[n], :], -1, keepdims=True)
+            att[x, rows[n], lanes[h]] = (acc_ref[h, rows[n], :] / norm).astype(bf16)
+            a_hop(0, h, n, x, x_right).start()
+            a_hop(1, h, n, x, x_left).start()
 
     finish(0)
     back(3)
@@ -628,7 +635,8 @@
         @pl.when(given)
         def _():
             for h in range(HEADS):
-                o_hop(s, h).wait_send()
+                for n in range(2):
+                    o_hop(s, h, n).wait_send()
                 s_hop(s, h).wait_send()
 
 
@@ -656,7 +664,7 @@
         scratch += [state, state, state, pltpu.VMEM((HEADS, tokens, tokens), f32)]
         scratch += [pltpu.VMEM((4,) + shard, bf16), pltpu.VMEM((4, width, width), bf16)]
         each, two, halves = (HEADS,), (2, HEADS), (2, HEADS, 2)
-        sems = [each] * 12 + [(), (), two, two, (2,), (2,), two, two, two, two]
+        sems = [each] * 12 + [(), (), two, two, (2,), (2,), halves, halves, two, two]
         sems += [(3,), (3,), (3,), (3,), halves, halves, two, two, (), (6,)]
         scratch += [dma(s) if s else dma for s in sems]
         return pl.pallas_call(

time: 47.8 us -> 47.3 us (0.990)
  no operation moved by 1% of the time
where the time goes in v5:
time: 47.3 us; the launch traced here: 47.2 us
  Pallas kernels  46.5 us (98%)
  local copies, waits for them, and re-layouts  0.71 us (2%)
    pallas_call x1, Pallas kernels, body(): pl.pallas_call(functools.partial(kernel, n_ctx), out_shape=pltpu.VMEM(sha...  46.5 us

profile of v5, /device:TPU:256, one launch (start us, length us, event | category | flops | bytes accessed | tf_op | source)
XLA Modules:
  0.0 47.2 jit_solution(12526299934465459785)
XLA Ops:
  0.0 46.5 %path_attention.1 = bf16[256,512]{1,0:T(8,128)(2,1)S(1)} custom-call(s32[2,4]{1,0:T(2,128)} %sel_hbm.1, bf16[256,512]{1,0:T(8,128)(2,1)} %q_hbm.1, bf16[256,512]{1,0:T(8,128)(2,1)} %k_hbm.1, bf16[256,512]{1,0:T(8,128)(2,1)} %v_hbm.1, bf16[256,512]{1,0:T(8,128)(2,1)} %w_hbm.1, f32[4,256]{1,0:T(4,128)} %rate_hbm.1, bf16[512,2048]{1,0:T(8,128)(2,1)} %ow_ref.1), custom_call_target="tpu_custom_call" | custom-call | tf_op jit(solution)/shard_map/path_attention/pallas_call | solution.py:670
  46.5 0.7 %copy.9 = bf16[256,512]{1,0:T(8,128)(2,1)} copy(bf16[256,512]{1,0:T(8,128)(2,1)S(1)} %path_attention.1) | data formatting | bytes 524288

commit v6 on v5

--- a/solution.py
+++ b/solution.py
@@ -183,8 +183,10 @@
             so.at[s, h, n], ro.at[s, h, n], (nxt, x),
         )
 
-    def s_hop(s, h):
-        return remote(s_out.at[s, h], s_in.at[s, h], ss.at[s, h], rs.at[s, h], (nxt, x))
+    def s_hop(s, h, n):
+        return remote(
+            s_out.at[s, h, n], s_in.at[s, h, n], ss.at[s, h, n], rs.at[s, h, n], (nxt, x)
+        )
 
     half = pl.ds(pl.multiple_of(core * 256, 256), 256)
     other_half = pl.ds(pl.multiple_of((1 - core) * 256, 256), 256)
@@ -391,27 +393,23 @@
         v_extra(h, v_own, cross).wait_recv()
         k_extra(h, k_tail, cross).wait_recv()
 
-    def result(g):
-        parts, logs = [], []
+    def give_half(s, h, n):
+        g = (s + 1) * HEADS + h
+        norm = jnp.sum(l_ref[g, rows[n], :], -1, keepdims=True)
+        o_out[s, rows[n], lanes[h]] = (acc_ref[g, rows[n], :] / norm).astype(bf16)
+        s_out[s, h, n, :, :] = jnp.transpose(m_ref[g, rows[n], :] + jnp.log(norm))[:1, :]
+        s_hop(s, h, n).start()
+        o_hop(s, h, n).start()
+
+    def give(s, h):
         for n in range(2):
-            norm = jnp.sum(l_ref[g, rows[n], :], -1, keepdims=True)
-            parts.append(acc_ref[g, rows[n], :] / norm)
-            logs.append(jnp.transpose(m_ref[g, rows[n], :] + jnp.log(norm))[:1, :])
-        return parts, logs
-
-    def give(s, h):
-        parts, logs = result((s + 1) * HEADS + h)
-        for n in range(2):
-            o_out[s, rows[n], lanes[h]] = parts[n].astype(bf16)
-            s_out[s, h, n : n + 1, :] = logs[n]
-        s_hop(s, h).start()
-        for n in range(2):
-            o_hop(s, h, n).start()
+            give_half(s, h, n)
 
     def merge(s, h, n):
         g = s * HEADS + h
+        s_hop(s, h, n).wait_recv()
         o_hop(s, h, n).wait_recv()
-        log = jnp.transpose(jnp.broadcast_to(s_in[s, h, n : n + 1, :], (B, B)))
+        log = jnp.transpose(jnp.broadcast_to(s_in[s, h, n, :, :], (B, B)))
         old = m_ref[g, rows[n], :]
         top = jnp.maximum(old, log)
         fade, weight = jnp.exp(old - top), jnp.exp(log - top)
@@ -420,11 +418,6 @@
         acc_ref[g, rows[n], :] = (
             acc_ref[g, rows[n], :] * fade + o_in[s, rows[n], lanes[h]].astype(f32) * weight
         )
-
-    def take(s, h):
-        s_hop(s, h).wait_recv()
-        for n in range(2):
-            merge(s, h, n)
 
     inputs[5].wait()
     for h in range(HEADS):
@@ -513,11 +506,13 @@
     def back(h):
         @pl.when(visit1)
         def _():
-            @pl.when(has_prev2)
-            def _():
-                take(1, h)
-
-            give(0, h)
+            for n in range(2):
+
+                @pl.when(has_prev2)
+                def _():
+                    merge(1, h, n)
+
+                give_half(0, h, n)
 
     @pl.when(visit2)
     def _():
@@ -550,8 +545,6 @@
 
             @pl.when(has_prev2)
             def _():
-                if n == 0:
-                    s_hop(0, h).wait_recv()
                 merge(0, h, n)
 
             norm = jnp.sum(l_ref[h, rows[n], :], -1, keepdims=True)
@@ -637,7 +630,8 @@
             for h in range(HEADS):
                 for n in range(2):
                     o_hop(s, h, n).wait_send()
-                s_hop(s, h).wait_send()
+                for n in range(2):
+                    s_hop(s, h, n).wait_send()
 
 
 def solution(mesh):
@@ -660,11 +654,11 @@
         scratch += [slab, slab, pair(shard, bf16), pair(shard, bf16)]
         scratch += [pltpu.VMEM((20, HD), f32), pair((20, HD), f32)]
         scratch += [pair(shard, bf16), pair(shard, bf16)]
-        scratch += [pair((HEADS, 2, HD), f32), pair((HEADS, 2, HD), f32)]
+        scratch += [pair((HEADS, 2, 1, HD), f32), pair((HEADS, 2, 1, HD), f32)]
         scratch += [state, state, state, pltpu.VMEM((HEADS, tokens, tokens), f32)]
         scratch += [pltpu.VMEM((4,) + shard, bf16), pltpu.VMEM((4, width, width), bf16)]
         each, two, halves = (HEADS,), (2, HEADS), (2, HEADS, 2)
-        sems = [each] * 12 + [(), (), two, two, (2,), (2,), halves, halves, two, two]
+        sems = [each] * 12 + [(), (), two, two, (2,), (2,), halves, halves, halves, halves]
         sems += [(3,), (3,), (3,), (3,), halves, halves, two, two, (), (6,)]
         scratch += [dma(s) if s else dma for s in sems]
         return pl.pallas_call(

time: 47.3 us -> 47.3 us (level)
  no operation moved by 1% of the time
where the time goes in v6:
time: 47.3 us; the launch traced here: 47.1 us
  Pallas kernels  46.4 us (98%)
  local copies, waits for them, and re-layouts  0.71 us (2%)
    pallas_call x1, Pallas kernels, body(): pl.pallas_call(functools.partial(kernel, n_ctx), out_shape=pltpu.VMEM(sha...  46.4 us

profile of v6, /device:TPU:256, one launch (start us, length us, event | category | flops | bytes accessed | tf_op | source)
XLA Modules:
  0.0 47.1 jit_solution(1226618778838829599)
XLA Ops:
  0.0 46.4 %path_attention.1 = bf16[256,512]{1,0:T(8,128)(2,1)S(1)} custom-call(s32[2,4]{1,0:T(2,128)} %sel_hbm.1, bf16[256,512]{1,0:T(8,128)(2,1)} %q_hbm.1, bf16[256,512]{1,0:T(8,128)(2,1)} %k_hbm.1, bf16[256,512]{1,0:T(8,128)(2,1)} %v_hbm.1, bf16[256,512]{1,0:T(8,128)(2,1)} %w_hbm.1, f32[4,256]{1,0:T(4,128)} %rate_hbm.1, bf16[512,2048]{1,0:T(8,128)(2,1)} %ow_ref.1), custom_call_target="tpu_custom_call" | custom-call | tf_op jit(solution)/shard_map/path_attention/pallas_call | solution.py:664
  46.4 0.7 %copy.9 = bf16[256,512]{1,0:T(8,128)(2,1)} copy(bf16[256,512]{1,0:T(8,128)(2,1)S(1)} %path_attention.1) | data formatting | bytes 524288
